TPU v7x, 32 devices: a whole 2x2x4 slice. The times are simulated.
32 devices in a mesh: seq: 16 (over z, y, core), dp: 2 (over x).
Axes of the slice: x: 2, y: 2, z: 4, core: 2. Of those that a mesh axis runs over, the one named last changes fastest.
Arguments:
- queries: bfloat16 [2, 4096, 2048], P('dp', 'seq'), may hold values from -6 to 6
- key_rows: bfloat16 [2, 4096, 2048], P('dp', 'seq'), may hold values from -6 to 6
- value_rows: bfloat16 [2, 4096, 2048], P('dp', 'seq'), may hold values from -6 to 6
- out_grad: bfloat16 [2, 4096, 2048], P('dp', 'seq'), may hold values from -6 to 6
- out_weight: bfloat16 [2048, 2048], P('seq', 'dp'), may hold values from -0.125 to 0.125
Outputs:
- query_grad: bfloat16 [2, 4096, 2048], P('dp', 'seq')
- key_grad: bfloat16 [2, 4096, 2048], P('dp', 'seq')
- value_grad: bfloat16 [2, 4096, 2048], P('dp', 'seq')
- weight_grad: float32 [2048, 2048], P('seq', 'dp')
All inputs are finite; a program needn't handle non-finite values.
Results may differ from a plain program's by a relative error of at most 0.014.
Values may be sent and summed in bfloat16 or wider, within the bound.
A program may use at most 192 MiB of HBM per device.

v0:
```python
import math

import jax
import jax.numpy as jnp
from jax import lax
from jax.sharding import PartitionSpec as P

HEADS = 16
HEAD = 128
HD = 2048


def prefix_2(part, axis, combine, identity, reverse):
    count = lax.axis_size(axis)
    place = lax.axis_index(axis)
    ahead = count - 1 - place if reverse else place
    gathered = lax.all_gather(part, axis)
    state = jnp.zeros_like(part) + jnp.asarray(identity, part.dtype)

    def one(step, state):
        source = count - 1 - step if reverse else step
        return combine(state, lax.dynamic_index_in_dim(gathered, source, 0, False))

    return lax.fori_loop(0, ahead, one, state)


def add_sums(earlier, later):
    return earlier + later


def shards(queries, key_rows, value_rows, out_grad, out_weight):
    tokens_dev = queries.shape[1]
    seq_devices = lax.axis_size("seq")
    data_devices = lax.axis_size("dp")
    seq_length = tokens_dev * seq_devices
    seq_count = queries.shape[0] * data_devices
    score_scale = 1.0 / math.sqrt(HEAD * seq_length)
    grad_scale = 1.0 / math.sqrt(seq_count * seq_length)
    query_flat = queries[0]
    grad_flat = out_grad[0]
    query_h = query_flat.reshape(tokens_dev, HEADS, HEAD)
    key_h = key_rows[0].reshape(tokens_dev, HEADS, HEAD)
    value_h = value_rows[0].reshape(tokens_dev, HEADS, HEAD)
    row_ids = lax.broadcasted_iota(jnp.int32, (tokens_dev, tokens_dev), 0)
    col_ids = lax.broadcasted_iota(jnp.int32, (tokens_dev, tokens_dev), 1)
    causal = (row_ids >= col_ids).astype(jnp.float32)
    empty_state = jnp.zeros((HEADS, HEAD, HEAD), jnp.float32)
    kv_local = jnp.einsum("shd,she->hde", key_h, value_h, preferred_element_type=jnp.float32)
    wide_weight = lax.all_gather(out_weight, "dp", axis=1, tiled=True)
    head_grad = lax.dot_general(
        grad_flat,
        lax.all_gather(wide_weight, "seq", axis=0, tiled=True),
        (((1,), (1,)), ((), ())),
        preferred_element_type=jnp.float32,
    ).astype(jnp.bfloat16)
    grad_h = head_grad.reshape(tokens_dev, HEADS, HEAD)
    query_dout = jnp.einsum("thd,the->hde", query_h, grad_h, preferred_element_type=jnp.float32)
    prefix = prefix_2(kv_local, "seq", add_sums, empty_state, False)
    suffix = prefix_2(query_dout, "seq", add_sums, empty_state, True)
    prefix_scaled = (score_scale * prefix).astype(jnp.bfloat16)
    suffix_scaled = (score_scale * suffix).astype(jnp.bfloat16)
    scores = (
        score_scale
        * jnp.einsum("thd,shd->hts", query_h, key_h, preferred_element_type=jnp.float32)
        * causal
    ).astype(jnp.bfloat16)
    attended = jnp.einsum("hts,shd->thd", scores, value_h, preferred_element_type=jnp.float32)
    attended = attended + jnp.einsum(
        "thd,hde->the", query_h, prefix_scaled, preferred_element_type=jnp.float32
    )
    attended = attended.astype(jnp.bfloat16).reshape(tokens_dev, HD)
    row_sums = lax.psum_scatter(
        (
            grad_scale
            * lax.dot_general(
                attended, grad_flat, (((0,), (0,)), ((), ())), preferred_element_type=jnp.float32
            )
        ).astype(jnp.bfloat16),
        "seq",
        scatter_dimension=0,
        tiled=True,
    )
    weight_grad = lax.psum_scatter(row_sums, "dp", scatter_dimension=1, tiled=True).astype(
        jnp.float32
    )
    grad_scores = (
        score_scale
        * jnp.einsum("the,she->hts", grad_h, value_h, preferred_element_type=jnp.float32)
        * causal
    ).astype(jnp.bfloat16)
    query_g = jnp.einsum("hts,shd->thd", grad_scores, key_h, preferred_element_type=jnp.float32)
    query_g = query_g + jnp.einsum(
        "the,hde->thd", grad_h, prefix_scaled, preferred_element_type=jnp.float32
    )
    key_g = jnp.einsum("hts,thd->shd", grad_scores, query_h, preferred_element_type=jnp.float32)
    key_g = key_g + jnp.einsum(
        "she,hde->shd", value_h, suffix_scaled, preferred_element_type=jnp.float32
    )
    value_g = jnp.einsum("hts,the->she", scores, grad_h, preferred_element_type=jnp.float32)
    value_g = value_g + jnp.einsum(
        "shd,hde->she", key_h, suffix_scaled, preferred_element_type=jnp.float32
    )
    query_grad = query_g.astype(jnp.bfloat16).reshape(1, tokens_dev, HD)
    key_grad = key_g.astype(jnp.bfloat16).reshape(1, tokens_dev, HD)
    value_grad = value_g.astype(jnp.bfloat16).reshape(1, tokens_dev, HD)
    return (query_grad, key_grad, value_grad, weight_grad)


def solution(mesh):
    return jax.shard_map(
        shards,
        mesh=mesh,
        in_specs=(
            P("dp", "seq", None),
            P("dp", "seq", None),
            P("dp", "seq", None),
            P("dp", "seq", None),
            P("seq", "dp"),
        ),
        out_specs=(
            P("dp", "seq", None),
            P("dp", "seq", None),
            P("dp", "seq", None),
            P("seq", "dp"),
        ),
        check_vma=False,
    )
```

profile of v0, /device:TPU:0, one launch (start us, length us, event | category | flops | bytes accessed | tf_op | source)
XLA Modules:
  0.0 536.6 jit_solution(13903750123057285457)
XLA Ops:
  7.2 1.6 copy.56
  8.8 1.8 copy.57
  16.0 2.2 fusion.22
  18.2 123.7 %all-gather.8.cloned.1.call-done = f32[256,128,128]{2,1,0:T(8,128)} async-done(((f32[16,128,128]{2,1,0:T(8,128)}), f32[256,128,128]{2,1,0:T(8,128)}) %all-gather.8.cloned.1.call-update) | async-done | bytes 16777232 | tf_op jit(solution)/shard_map/all_gather | solution.py:17
  142.0 2.5 fusion
  144.5 5.7 %multiply_convert_fusion = bf16[2048,2048]{1,0:T(8,128)(2,1)} fusion(bf16[256,2048]{0,1:T(8,128)(2,1)S(1)} %bitcast.84, bf16[1,256,2048]{2,1,0:T(8,128)(2,1)S(1)} %copy-done), kind=kOutput, calls=%fused_computation.2 | convolution fusion | flops 2155872256 | bytes 10485760 | tf_op jit(solution)/shard_map/dot_general | solution.py:75
  150.2 10.2 %all_gather.18 = bf16[128,2048]{1,0:T(8,128)(2,1)} all-gather(bf16[128,1024]{1,0:T(8,128)(2,1)} %param.13), channel_id=1, replica_groups=mesh['seq'=16,'dp'=2] {'dp'}, dimensions={1}, use_global_device_ids=true | all-gather | bytes 786432 | tf_op jit(solution)/shard_map/all_gather | solution.py:49
  160.5 115.1 %reduce-scatter.3.cloned.1.call-done = bf16[128,2048]{1,0:T(8,128)(2,1)} async-done(((bf16[2048,2048]{1,0:T(8,128)(2,1)}), bf16[128,2048]{1,0:T(8,128)(2,1)}) %reduce-scatter.3.cloned.1.call-update) | async-done | bytes 524304 | tf_op jit(solution)/shard_map/reduce_scatter | solution.py:72
  275.9 76.6 %all-gather.6.cloned.1.call-done = bf16[2048,2048]{1,0:T(8,128)(2,1)} async-done(((bf16[128,2048]{1,0:T(8,128)(2,1)}), bf16[2048,2048]{1,0:T(8,128)(2,1)}) %all-gather.6.cloned.1.call-update) | async-done | bytes 8388624 | tf_op jit(solution)/shard_map/all_gather | solution.py:52
  352.5 6.8 %convolution_convert_fusion = bf16[256,2048]{1,0:T(8,128)(2,1)} fusion(bf16[2048,2048]{1,0:T(8,128)(2,1)} %all-gather.6.cloned.1.call-done, bf16[1,256,2048]{2,1,0:T(8,128)(2,1)S(1)} %copy-done), kind=kOutput, calls=%fused_computation.5 | convolution fusion | flops 2148007936 | bytes 10485760 | tf_op jit(solution)/shard_map/dot_general | solution.py:50
  359.2 2.3 copy.55
  361.6 2.7 convolution_bitcast_fusion
  364.2 2.7 copy.40
  366.9 2.0 multiply_convert_fusion.2
  370.2 1.9 fusion.11
  372.9 1.8 fusion.21
  376.1 2.3 copy.50
  378.4 1.8 convert_element_type.52
  380.2 116.4 %all-gather.10.cloned.1.call-done = f32[256,128,128]{2,1,0:T(8,128)} async-done(((f32[16,128,128]{2,1,0:T(8,128)}), f32[256,128,128]{2,1,0:T(8,128)}) %all-gather.10.cloned.1.call-update) | async-done | bytes 16777232 | tf_op jit(solution)/shard_map/all_gather | solution.py:17
  496.7 22.7 %while.23 = (s32[]{:T(128)}, f32[16,128,128]{2,1,0:T(8,128)S(1)}, s32[]{:T(128)}, f32[16,16,128,128]{3,2,1,0:T(8,128)}, s32[]{:T(128)}, /*index=5*/s32[]{:T(128)}, s32[]{:T(128)}, s32[]{:T(128)}) while((s32[]{:T(128)}, f32[16,128,128]{2,1,0:T(8,128)S(1)}, s32[]{:T(128)}, f32[16,16,128,128]{3,2,1,0:T(8,128)}, s32[]{:T(128)}, ...), condition=%wide.region_3.4_spmd, body=%wide.region_2.3_spmd.sunk | while | flops 262150 | bytes 3145871 | solution.py:24
  496.7 1.5 bitcast_add_fusion.8
  498.2 1.5 bitcast_add_fusion.8
  499.7 1.5 bitcast_add_fusion.8
  501.2 1.5 bitcast_add_fusion.8
  502.7 1.5 bitcast_add_fusion.8
  504.2 1.5 bitcast_add_fusion.8
  505.8 1.5 bitcast_add_fusion.8
  507.3 1.5 bitcast_add_fusion.8
  519.3 3.0 fusion.1
  522.3 2.3 copy.51
  524.6 3.2 add_convert_fusion
  527.8 2.3 copy.52
  (47 shorter events, 19.8 us)
Async XLA Ops:
  7.2 137.3 %copy-start = (bf16[1,256,2048]{2,1,0:T(8,128)(2,1)S(1)}, bf16[1,256,2048]{2,1,0:T(8,128)(2,1)}, u32[]{:S(2)}) copy-start(bf16[1,256,2048]{2,1,0:T(8,128)(2,1)} %param.12) | copy-start | bytes 3145732
  7.2 134.7 %all-gather.8.cloned.1.call-start = ((), (), s32[]{:S(2)}) async-start(), calls=%async_computation.5 | async-start | bytes 17825792 | tf_op jit(solution)/shard_map/all_gather | solution.py:17
  8.8 5.6 %copy-start.2 = (bf16[1,256,2048]{1,2,0:T(8,128)(2,1)}, bf16[1,256,2048]{1,2,0:T(8,128)(2,1)S(1)}, u32[]{:S(2)}) copy-start(bf16[1,256,2048]{1,2,0:T(8,128)(2,1)S(1)} %copy.56) | copy-start | bytes 3145732
  12.1 263.5 %reduce-scatter.3.cloned.1.call-start = ((), (), s32[]{:S(2)}) async-start(), calls=%async_computation.3 | async-start | bytes 8912896 | tf_op jit(solution)/shard_map/reduce_scatter | solution.py:72
  13.6 1.0 copy-start.4
  14.6 1.3 copy-start.8
  150.2 202.3 %all-gather.6.cloned.1.call-start = ((), (), s32[]{:S(2)}) async-start(), calls=%async_computation.2 | async-start | bytes 8912896 | tf_op jit(solution)/shard_map/all_gather | solution.py:52
  160.5 217.9 %reduce-scatter.5.cloned.1.call-start = ((), (), s32[]{:S(2)}) async-start(), calls=%async_computation.4 | async-start | bytes 786432 | tf_op jit(solution)/shard_map/reduce_scatter | solution.py:83
  275.6 220.9 %all-gather.10.cloned.1.call-start = ((), (), s32[]{:S(2)}) async-start(), calls=%async_computation.6 | async-start | bytes 17825792 | tf_op jit(solution)/shard_map/all_gather | solution.py:17
  359.2 2.4 copy-start.5
  364.2 2.7 copy-start.3
  368.9 1.2 copy-start.6
  370.2 1.9 copy-start.7
  370.2 2.7 copy-start.9
  524.6 5.5 %copy-start.1 = (bf16[1,256,2048]{2,1,0:T(8,128)(2,1)S(1)}, bf16[1,256,2048]{2,1,0:T(8,128)(2,1)}, u32[]{:S(2)}) copy-start(bf16[1,256,2048]{2,1,0:T(8,128)(2,1)} %param.12) | copy-start | bytes 3145732
Sparse Core Ops, SparseCore 0:
  12.2 129.5 all-gather.7
  150.3 125.2 reduce-scatter.2
  277.8 74.6 all-gather.5
  354.6 12.7 reduce-scatter.4
  369.6 126.8 all-gather.9
where the time goes:
time: 538 us; the launch traced here: 537 us
  waiting for transfers between devices  432 us (80%)
  matrix products  36 us (7%)
  other arithmetic  24.1 us (4%)
  local copies, waits for them, and re-layouts  19.7 us (4%)
  between operations  13.9 us (3%)
  blocking collectives  10.2 us (2%)
    all_gather x2, waiting for transfers between devices, prefix_2(): gathered = lax.all_gather(part, axis)  240 us
    reduce_scatter x1, waiting for transfers between devices, shards(): lax.psum_scatter((grad_scale * lax.dot_general(attended, grad_flat, (((0,...  115 us
    all_gather x1, waiting for transfers between devices, shards(): lax.all_gather(wide_weight, 'seq', axis=0, tiled=True)  76.6 us
    add x15, other arithmetic, add_sums(): return earlier + later  22.3 us
    unnamed x25, local copies, waits for them, and re-layouts  12.9 us
  transfers between devices with their start and end apart: 5, of which 4 were waited for; matrix products, arithmetic and copies ran while one was open for 6% of the time, Pallas kernels for 0%

commit v1 on v0

--- a/solution.py
+++ b/solution.py
@@ -10,22 +10,20 @@
 HD = 2048
 
 
-def prefix_2(part, axis, combine, identity, reverse):
+def exchanged_sums(part, scale, axis, reverse):
     count = lax.axis_size(axis)
-    place = lax.axis_index(axis)
-    ahead = count - 1 - place if reverse else place
-    gathered = lax.all_gather(part, axis)
-    state = jnp.zeros_like(part) + jnp.asarray(identity, part.dtype)
-
-    def one(step, state):
-        source = count - 1 - step if reverse else step
-        return combine(state, lax.dynamic_index_in_dim(gathered, source, 0, False))
-
-    return lax.fori_loop(0, ahead, one, state)
-
-
-def add_sums(earlier, later):
-    return earlier + later
+    heads, depth, width = part.shape
+    rows = part.reshape(heads * depth, width).astype(jnp.bfloat16)
+    mine = lax.all_to_all(rows, axis, 0, 0, tiled=True)
+    mine = mine.reshape(count, -1, width).astype(jnp.float32)
+    order = range(count - 1, -1, -1) if reverse else range(count)
+    state = jnp.zeros_like(mine[0])
+    sums = [None] * count
+    for source in order:
+        sums[source] = (scale * state).astype(jnp.bfloat16)
+        state = state + mine[source]
+    back = lax.all_to_all(jnp.concatenate(sums, axis=0), axis, 0, 0, tiled=True)
+    return back.reshape(heads, depth, width)
 
 
 def shards(queries, key_rows, value_rows, out_grad, out_weight):
@@ -44,7 +42,6 @@
     row_ids = lax.broadcasted_iota(jnp.int32, (tokens_dev, tokens_dev), 0)
     col_ids = lax.broadcasted_iota(jnp.int32, (tokens_dev, tokens_dev), 1)
     causal = (row_ids >= col_ids).astype(jnp.float32)
-    empty_state = jnp.zeros((HEADS, HEAD, HEAD), jnp.float32)
     kv_local = jnp.einsum("shd,she->hde", key_h, value_h, preferred_element_type=jnp.float32)
     wide_weight = lax.all_gather(out_weight, "dp", axis=1, tiled=True)
     head_grad = lax.dot_general(
@@ -55,10 +52,8 @@
     ).astype(jnp.bfloat16)
     grad_h = head_grad.reshape(tokens_dev, HEADS, HEAD)
     query_dout = jnp.einsum("thd,the->hde", query_h, grad_h, preferred_element_type=jnp.float32)
-    prefix = prefix_2(kv_local, "seq", add_sums, empty_state, False)
-    suffix = prefix_2(query_dout, "seq", add_sums, empty_state, True)
-    prefix_scaled = (score_scale * prefix).astype(jnp.bfloat16)
-    suffix_scaled = (score_scale * suffix).astype(jnp.bfloat16)
+    prefix_scaled = exchanged_sums(kv_local, score_scale, "seq", False)
+    suffix_scaled = exchanged_sums(query_dout, score_scale, "seq", True)
     scores = (
         score_scale
         * jnp.einsum("thd,shd->hts", query_h, key_h, preferred_element_type=jnp.float32)

time: 538 us -> 320 us (0.59)
  waiting for transfers between devices: 432 us -> 203 us
  starting transfers between devices: 0.38 us -> 20.5 us
  other arithmetic: 24.1 us -> 13.8 us
    all_gather x2 -> x0, waiting for transfers between devices: 240 us -> none  [prefix_2(): gathered = lax.all_gather(part, axis)]
    all_to_all x0 -> x4, waiting for transfers between devices: none -> 32.4 us  [the longest x2 21.1 us: exchanged_sums(): mine = lax.all_to_all(rows, axis, 0, 0, tiled=True)]
    add x15 -> x0, other arithmetic: 22.3 us -> none  [add_sums(): return earlier + later]
    reduce_scatter x1, waiting for transfers between devices: 115 us -> 93.4 us  [shards(): lax.psum_scatter((grad_scale * lax.dot_general(attended, grad_flat, (((0,...]
    all_to_all x0 -> x4, starting transfers between devices: none -> 20.4 us  [the longest x2 11.7 us: exchanged_sums(): mine = lax.all_to_all(rows, axis, 0, 0, tiled=True)]
    unnamed x0 -> x29, other arithmetic: none -> 9.13 us
    unnamed x25 -> x20, local copies, waits for them, and re-layouts: 12.9 us -> 13.3 us
  transfers between devices with their start and end apart: 5 -> 7, of which waited for: 4 -> 6; matrix products, arithmetic and copies ran while one was open for 6% -> 11% of each run, Pallas kernels for 0% -> 0%
where the time goes in v1:
time: 320 us; the launch traced here: 319 us
  waiting for transfers between devices  203 us (63%)
  matrix products  40.6 us (13%)
  starting transfers between devices  20.5 us (6%)
  local copies, waits for them, and re-layouts  17 us (5%)
  between operations  14 us (4%)
  other arithmetic  13.8 us (4%)
  blocking collectives  10.6 us (3%)
    reduce_scatter x1, waiting for transfers between devices, shards(): lax.psum_scatter((grad_scale * lax.dot_general(attended, grad_flat, (((0,...  93.4 us
    all_gather x1, waiting for transfers between devices, shards(): lax.all_gather(wide_weight, 'seq', axis=0, tiled=True)  76.8 us
    all_to_all x2, waiting for transfers between devices, exchanged_sums(): mine = lax.all_to_all(rows, axis, 0, 0, tiled=True)  21.1 us
    unnamed x20, local copies, waits for them, and re-layouts  13.3 us
    all_to_all x2, starting transfers between devices, exchanged_sums(): mine = lax.all_to_all(rows, axis, 0, 0, tiled=True)  11.7 us
    all_to_all x2, waiting for transfers between devices, exchanged_sums(): back = lax.all_to_all(jnp.concatenate(sums, axis=0), axis, 0, 0, tiled=True)  11.3 us
    all_gather x1, blocking collectives, shards(): wide_weight = lax.all_gather(out_weight, 'dp', axis=1, tiled=True)  10.6 us
    unnamed x29, other arithmetic  9.13 us
  transfers between devices with their start and end apart: 7, of which 6 were waited for; matrix products, arithmetic and copies ran while one was open for 11% of the time, Pallas kernels for 0%

profile of v1, /device:TPU:0, one launch (start us, length us, event | category | flops | bytes accessed | tf_op | source)
XLA Modules:
  0.0 319.2 jit_solution(4573787005507438147)
XLA Ops:
  7.2 1.5 copy.36
  8.7 1.5 copy.35
  11.5 7.4 %all-to-all-start = ((bf16[16,128,128]{2,1,0:T(8,128)(2,1)}), bf16[16,128,128]{2,1,0:T(8,128)(2,1)}, u32[]{:S(2)}, u32[]{:S(2)}) async-start(bf16[16,128,128]{2,1,0:T(8,128)(2,1)} %convolution_convert_fusion.2), calls=%async_computation | async-start | bytes 1048576 | tf_op jit(solution)/shard_map/all_to_all | solution.py:17
  19.6 13.9 %all-to-all-done = bf16[16,128,128]{2,1,0:T(8,128)(2,1)} async-done(((bf16[16,128,128]{2,1,0:T(8,128)(2,1)}), bf16[16,128,128]{2,1,0:T(8,128)(2,1)}, u32[]{:S(2)}, u32[]{:S(2)}) %all-to-all-start) | async-done | bytes 524320 | tf_op jit(solution)/shard_map/all_to_all | solution.py:17
  44.0 4.2 %all-to-all-start.1 = ((bf16[16,128,128]{2,1,0:T(8,128)(2,1)}), bf16[16,128,128]{2,1,0:T(8,128)(2,1)}, u32[]{:S(2)}, u32[]{:S(2)}) async-start(bf16[16,128,128]{2,1,0:T(8,128)(2,1)} %bitcast.201), calls=%async_computation.1 | async-start | bytes 1048576 | tf_op jit(solution)/shard_map/all_to_all | solution.py:25
  48.3 1.5 copy.37
  50.8 1.3 copy-done.3
  52.1 2.2 fusion.52
  54.3 8.4 %all-to-all-done.1 = bf16[16,128,128]{2,1,0:T(8,128)(2,1)} async-done(((bf16[16,128,128]{2,1,0:T(8,128)(2,1)}), bf16[16,128,128]{2,1,0:T(8,128)(2,1)}, u32[]{:S(2)}, u32[]{:S(2)}) %all-to-all-start.1) | async-done | bytes 524320 | tf_op jit(solution)/shard_map/all_to_all | solution.py:25
  62.7 2.6 fusion
  65.3 5.6 %multiply_convert_fusion = bf16[2048,2048]{1,0:T(8,128)(2,1)} fusion(bf16[256,2048]{0,1:T(8,128)(2,1)S(1)} %bitcast.200, bf16[1,256,2048]{2,1,0:T(8,128)(2,1)S(1)} %copy-done), kind=kOutput, calls=%fused_computation | convolution fusion | flops 2155872256 | bytes 10485760 | tf_op jit(solution)/shard_map/dot_general | solution.py:70
  71.0 10.6 %all_gather.6 = bf16[128,2048]{1,0:T(8,128)(2,1)} all-gather(bf16[128,1024]{1,0:T(8,128)(2,1)} %param.9), channel_id=1, replica_groups=mesh['seq'=16,'dp'=2] {'dp'}, dimensions={1}, use_global_device_ids=true | all-gather | bytes 786432 | tf_op jit(solution)/shard_map/all_gather | solution.py:46
  81.7 93.4 %reduce-scatter.3.cloned.1.call-done = bf16[128,2048]{1,0:T(8,128)(2,1)} async-done(((bf16[2048,2048]{1,0:T(8,128)(2,1)}), bf16[128,2048]{1,0:T(8,128)(2,1)}) %reduce-scatter.3.cloned.1.call-update) | async-done | bytes 524304 | tf_op jit(solution)/shard_map/reduce_scatter | solution.py:67
  175.1 76.8 %all-gather.2.cloned.1.call-done = bf16[2048,2048]{1,0:T(8,128)(2,1)} async-done(((bf16[128,2048]{1,0:T(8,128)(2,1)}), bf16[2048,2048]{1,0:T(8,128)(2,1)}) %all-gather.2.cloned.1.call-update) | async-done | bytes 8388624 | tf_op jit(solution)/shard_map/all_gather | solution.py:49
  251.9 6.7 %convolution_convert_fusion = bf16[256,2048]{1,0:T(8,128)(2,1)} fusion(bf16[2048,2048]{1,0:T(8,128)(2,1)} %all-gather.2.cloned.1.call-done, bf16[1,256,2048]{2,1,0:T(8,128)(2,1)S(1)} %copy-done), kind=kOutput, calls=%fused_computation.3 | convolution fusion | flops 2148007936 | bytes 10485760 | tf_op jit(solution)/shard_map/dot_general | solution.py:47
  258.6 2.3 copy.34
  260.9 2.8 fusion.3
  263.7 4.3 %all-to-all-start.2 = ((bf16[16,128,128]{2,1,0:T(8,128)(2,1)}), bf16[16,128,128]{2,1,0:T(8,128)(2,1)}, u32[]{:S(2)}, u32[]{:S(2)}) async-start(bf16[16,128,128]{2,1,0:T(8,128)(2,1)} %fusion.3), calls=%async_computation.2 | async-start | bytes 1048576 | tf_op jit(solution)/shard_map/all_to_all | solution.py:17
  268.0 1.8 convert_element_type.204
  269.8 2.0 multiply_convert_fusion.2
  273.1 2.1 fusion.7
  275.2 7.2 %all-to-all-done.2 = bf16[16,128,128]{2,1,0:T(8,128)(2,1)} async-done(((bf16[16,128,128]{2,1,0:T(8,128)(2,1)}), bf16[16,128,128]{2,1,0:T(8,128)(2,1)}, u32[]{:S(2)}, u32[]{:S(2)}) %all-to-all-start.2) | async-done | bytes 524320 | tf_op jit(solution)/shard_map/all_to_all | solution.py:17
  284.8 4.4 %all-to-all-start.3 = ((bf16[16,128,128]{2,1,0:T(8,128)(2,1)}), bf16[16,128,128]{2,1,0:T(8,128)(2,1)}, u32[]{:S(2)}, u32[]{:S(2)}) async-start(bf16[16,128,128]{2,1,0:T(8,128)(2,1)} %bitcast.202), calls=%async_computation.3 | async-start | bytes 1048576 | tf_op jit(solution)/shard_map/all_to_all | solution.py:25
  289.3 3.5 %fusion.2 = bf16[256,16,128]{0,2,1:T(8,128)(2,1)} fusion(f32[16,256,128]{1,2,0:T(8,128)} %fusion.7, bf16[16,128,128]{2,1,0:T(8,128)(2,1)} %all-to-all-done.1, bf16[256,16,128]{0,2,1:T(8,128)(2,1)} %bitcast.193), kind=kOutput, calls=%fused_computation.9 | convolution fusion | flops 135266304 | bytes 4718592 | tf_op jit(solution)/shard_map/the,hde->thd/dot_general | solution.py:87
  292.7 2.3 copy.28
  295.0 3.8 %fusion.51 = f32[16,128,256]{2,1,0:T(8,128)} fusion(bf16[256,16,128]{0,2,1:T(8,128)(2,1)} %bitcast.194, bf16[16,256,256]{2,1,0:T(8,128)(2,1)} %copy-done.3), kind=kOutput, calls=%fused_computation.150 | convolution fusion | flops 268435456 | bytes 5242880 | tf_op jit(solution)/shard_map/hts,the->she/dot_general | solution.py:94
  298.8 1.9 fusion.11
  300.7 2.8 all-to-all-done.3
  303.5 3.2 %add_convert_fusion = bf16[16,128,256]{2,1,0:T(8,128)(2,1)} fusion(f32[16,128,256]{2,1,0:T(8,128)} %fusion.51, bf16[16,128,128]{2,1,0:T(8,128)(2,1)} %all-to-all-done.3, bf16[256,16,128]{2,1,0:T(8,128)(2,1)S(1)} %bitcast.186), kind=kOutput, calls=%fused_computation.10 | convolution fusion | flops 135266304 | bytes 4718592 | tf_op jit(solution)/shard_map/shd,hde->she/dot_general | solution.py:95
  306.8 2.3 copy.30
  309.1 2.2 fusion.1
  311.3 1.4 copy.29
  (57 shorter events, 17.3 us)
Async XLA Ops:
  7.2 58.2 %copy-start = (bf16[1,256,2048]{2,1,0:T(8,128)(2,1)S(1)}, bf16[1,256,2048]{2,1,0:T(8,128)(2,1)}, u32[]{:S(2)}) copy-start(bf16[1,256,2048]{2,1,0:T(8,128)(2,1)} %param.8) | copy-start | bytes 3145732
  11.5 22.0 %all-to-all-start = ((bf16[16,128,128]{2,1,0:T(8,128)(2,1)}), bf16[16,128,128]{2,1,0:T(8,128)(2,1)}, u32[]{:S(2)}, u32[]{:S(2)}) async-start(bf16[16,128,128]{2,1,0:T(8,128)(2,1)} %convolution_convert_fusion.2), calls=%async_computation | async-start | bytes 1048576 | tf_op jit(solution)/shard_map/all_to_all | solution.py:17
  44.0 18.7 %all-to-all-start.1 = ((bf16[16,128,128]{2,1,0:T(8,128)(2,1)}), bf16[16,128,128]{2,1,0:T(8,128)(2,1)}, u32[]{:S(2)}, u32[]{:S(2)}) async-start(bf16[16,128,128]{2,1,0:T(8,128)(2,1)} %bitcast.201), calls=%async_computation.1 | async-start | bytes 1048576 | tf_op jit(solution)/shard_map/all_to_all | solution.py:25
  48.3 126.8 %reduce-scatter.3.cloned.1.call-start = ((), (), s32[]{:S(2)}) async-start(), calls=%async_computation.7 | async-start | bytes 8912896 | tf_op jit(solution)/shard_map/reduce_scatter | solution.py:67
  49.8 1.0 copy-start.1
  50.8 1.3 copy-start.3
  70.9 181.0 %all-gather.2.cloned.1.call-start = ((), (), s32[]{:S(2)}) async-start(), calls=%async_computation.6 | async-start | bytes 8912896 | tf_op jit(solution)/shard_map/all_gather | solution.py:49
  81.7 186.3 %reduce-scatter.5.cloned.1.call-start = ((), (), s32[]{:S(2)}) async-start(), calls=%async_computation.8 | async-start | bytes 786432 | tf_op jit(solution)/shard_map/reduce_scatter | solution.py:78
  263.7 18.7 %all-to-all-start.2 = ((bf16[16,128,128]{2,1,0:T(8,128)(2,1)}), bf16[16,128,128]{2,1,0:T(8,128)(2,1)}, u32[]{:S(2)}, u32[]{:S(2)}) async-start(bf16[16,128,128]{2,1,0:T(8,128)(2,1)} %fusion.3), calls=%async_computation.2 | async-start | bytes 1048576 | tf_op jit(solution)/shard_map/all_to_all | solution.py:17
  271.8 1.3 copy-start.4
  284.0 0.8 copy-start.6
  284.8 18.7 %all-to-all-start.3 = ((bf16[16,128,128]{2,1,0:T(8,128)(2,1)}), bf16[16,128,128]{2,1,0:T(8,128)(2,1)}, u32[]{:S(2)}, u32[]{:S(2)}) async-start(bf16[16,128,128]{2,1,0:T(8,128)(2,1)} %bitcast.202), calls=%async_computation.3 | async-start | bytes 1048576 | tf_op jit(solution)/shard_map/all_to_all | solution.py:25
  295.0 3.8 %copy-start.2 = (bf16[32,8,16,128]{3,2,1,0:T(8,128)(2,1)S(1)}, bf16[32,8,16,128]{3,2,1,0:T(8,128)(2,1)}, u32[]{:S(2)}) copy-start(bf16[32,8,16,128]{3,2,1,0:T(8,128)(2,1)} %copy-done.1) | copy-start | bytes 3145732
  295.0 3.8 %copy-start.5 = (bf16[16,256,256]{2,1,0:T(8,128)(2,1)S(1)}, bf16[16,256,256]{2,1,0:T(8,128)(2,1)}, u32[]{:S(2)}) copy-start(bf16[16,256,256]{2,1,0:T(8,128)(2,1)} %copy-done.4) | copy-start | bytes 6291460
Sparse Core Ops, SparseCore 0:
  71.1 103.9 reduce-scatter.2
  177.2 74.6 all-gather.1
  254.2 12.7 reduce-scatter.4

commit v2 on v1

--- a/solution.py
+++ b/solution.py
@@ -1,8 +1,11 @@
+import functools
 import math
 
 import jax
 import jax.numpy as jnp
 from jax import lax
+from jax.experimental import pallas as pl
+from jax.experimental.pallas import tpu as pltpu
 from jax.sharding import PartitionSpec as P
 
 HEADS = 16
@@ -15,15 +18,249 @@
     heads, depth, width = part.shape
     rows = part.reshape(heads * depth, width).astype(jnp.bfloat16)
     mine = lax.all_to_all(rows, axis, 0, 0, tiled=True)
-    mine = mine.reshape(count, -1, width).astype(jnp.float32)
-    order = range(count - 1, -1, -1) if reverse else range(count)
-    state = jnp.zeros_like(mine[0])
-    sums = [None] * count
-    for source in order:
-        sums[source] = (scale * state).astype(jnp.bfloat16)
-        state = state + mine[source]
-    back = lax.all_to_all(jnp.concatenate(sums, axis=0), axis, 0, 0, tiled=True)
+    mine = mine.reshape(count, -1)
+    ids = jnp.arange(count)
+    ahead = ids[:, None] < ids[None, :] if reverse else ids[:, None] > ids[None, :]
+    sums = jnp.dot(ahead.astype(jnp.bfloat16), mine, preferred_element_type=jnp.float32)
+    sums = (scale * sums).astype(jnp.bfloat16).reshape(-1, width)
+    back = lax.all_to_all(sums, axis, 0, 0, tiled=True)
     return back.reshape(heads, depth, width)
+
+
+STREAMS = 4
+MESH = pl.DeviceIdType.MESH
+
+
+def log2(count):
+    return count.bit_length() - 1
+
+
+def stream_bits(stream, seq_count, data_count):
+    high = [("seq", bit) for bit in range(log2(seq_count) - 1, 0, -1)]
+    data = [("dp", bit) for bit in range(log2(data_count))]
+    return high[:-1] + data + high[-1:] if stream % 2 else high + data
+
+
+def place(bits, seq, data):
+    index = {"seq": seq, "dp": data}
+    return sum((index[axis] // 2**bit) % 2 * 2**level for level, (axis, bit) in enumerate(bits))
+
+
+def partner(axis, bit):
+    index = lax.axis_index(axis)
+    return {axis: index + (1 - 2 * ((index // 2**bit) % 2)) * 2**bit}
+
+
+def greet(seq_count, data_count):
+    barrier = pltpu.get_barrier_semaphore()
+    bits = [("seq", 0)] + stream_bits(0, seq_count, data_count)
+    for axis, bit in bits:
+        pl.semaphore_signal(barrier, inc=1, device_id=partner(axis, bit), device_id_type=MESH)
+    pl.semaphore_wait(barrier, len(bits))
+
+
+def remote(src, dst, send, recv, device):
+    return pltpu.make_async_remote_copy(
+        src_ref=src, dst_ref=dst, send_sem=send, recv_sem=recv, device_id=device, device_id_type=MESH
+    )
+
+
+def head_grad_kernel(
+    seq_count, data_count, weight_ref, grad_ref, out_ref,
+    held, sib_grad, away, landed, send_sem, recv_sem, pair_send, pair_recv,
+):
+    seq, data = lax.axis_index("seq"), lax.axis_index("dp")
+    core = seq % 2
+    sibling = partner("seq", 0)
+    rows = held.shape[2]
+    orders = [stream_bits(s, seq_count, data_count) for s in range(STREAMS)]
+    slots = [place(orders[s], seq, data) for s in range(STREAMS)]
+    levels = len(orders[0])
+    for s in range(STREAMS):
+        held[s, slots[s]] = weight_ref[s * rows : (s + 1) * rows, :]
+    greet(seq_count, data_count)
+
+    def hop(s, level):
+        size = 2**level
+        block = held.at[s, pl.ds(slots[s] // size * size, size)]
+        axis, bit = orders[s][level]
+        return remote(
+            block, block, send_sem.at[s, level], recv_sem.at[s, level], partner(axis, bit)
+        )
+
+    for s in range(STREAMS):
+        hop(s, 0).start()
+    swap = remote(grad_ref, sib_grad, pair_send.at[0], pair_recv.at[0], sibling)
+    swap.start()
+    for level in range(levels):
+        for s in range(STREAMS):
+            hop(s, level).wait()
+            if level + 1 < levels:
+                hop(s, level + 1).start()
+    swap.wait()
+
+    group = max(1, 256 // (rows * STREAMS))
+    width = group * rows * STREAMS
+    for first in range(0, seq_count // 2, group):
+        panel = jnp.concatenate(
+            [
+                jnp.concatenate(
+                    [held[s, place(orders[s], 2 * j, d)] for d in range(data_count)], axis=1
+                )
+                for j in range(first, first + group)
+                for s in range(STREAMS)
+            ],
+            axis=0,
+        )
+        columns = slice(first // group * width, (first // group + 1) * width)
+        for source, target in ((grad_ref, out_ref.at[core]), (sib_grad, away)):
+            target[:, columns] = lax.dot_general(
+                source[...], panel, (((1,), (1,)), ((), ())), preferred_element_type=jnp.float32
+            ).astype(jnp.bfloat16)
+    back = remote(away, landed, pair_send.at[1], pair_recv.at[1], sibling)
+    back.start()
+    back.wait()
+    out_ref[1 - core] = landed[...]
+
+
+def gathered_head_grad(weight, grad, seq_count, data_count):
+    tokens, features = grad.shape[0], weight.shape[0] * seq_count
+    levels = log2(seq_count // 2) + log2(data_count)
+    half = (tokens, features // 2)
+    vmem = pl.BlockSpec(memory_space=pltpu.VMEM)
+    return pl.pallas_call(
+        functools.partial(head_grad_kernel, seq_count, data_count),
+        out_shape=jax.ShapeDtypeStruct((2,) + half, jnp.bfloat16),
+        in_specs=[vmem] * 2,
+        out_specs=vmem,
+        scratch_shapes=[
+            pltpu.VMEM(
+                (STREAMS, 2**levels, weight.shape[0] // STREAMS, weight.shape[1]), jnp.bfloat16
+            ),
+            pltpu.VMEM(grad.shape, jnp.bfloat16),
+            pltpu.VMEM(half, jnp.bfloat16),
+            pltpu.VMEM(half, jnp.bfloat16),
+            pltpu.SemaphoreType.DMA((STREAMS, levels)),
+            pltpu.SemaphoreType.DMA((STREAMS, levels)),
+            pltpu.SemaphoreType.DMA((2,)),
+            pltpu.SemaphoreType.DMA((2,)),
+        ],
+        compiler_params=pltpu.CompilerParams(
+            collective_id=0, has_side_effects=True, vmem_limit_bytes=40 << 20
+        ),
+        cost_estimate=pl.CostEstimate(
+            flops=2 * tokens * features * grad.shape[1],
+            bytes_accessed=150 << 20,
+            transcendentals=0,
+        ),
+    )(weight, grad)
+
+
+def weight_grad_kernel(
+    seq_count, data_count, scale, att_ref, grad_ref, out_ref,
+    sums, arrived, sib_att, sib_grad, send_sem, recv_sem, pair_send, pair_recv,
+):
+    seq, data = lax.axis_index("seq"), lax.axis_index("dp")
+    core = seq % 2
+    sibling = partner("seq", 0)
+    rows, columns = sums.shape[2], sums.shape[3]
+    orders = [stream_bits(s, seq_count, data_count) for s in range(STREAMS)]
+    slots = [place(orders[s], seq, data) for s in range(STREAMS)]
+    levels = len(orders[0])
+    greet(seq_count, data_count)
+    swaps = [
+        remote(att_ref.at[1 - core], sib_att, pair_send.at[0], pair_recv.at[0], sibling),
+        remote(grad_ref, sib_grad, pair_send.at[1], pair_recv.at[1], sibling),
+    ]
+    for swap in swaps:
+        swap.start()
+    for swap in swaps:
+        swap.wait()
+
+    group = max(1, 256 // (rows * STREAMS))
+    height = group * rows * STREAMS
+    for first in range(0, seq_count // 2, group):
+        part = pl.ds(first * rows * STREAMS, height)
+        for d in range(data_count):
+            across = slice(d * columns, (d + 1) * columns)
+            panel = jnp.dot(
+                att_ref[core, part, :], grad_ref[:, across], preferred_element_type=jnp.float32
+            )
+            panel = panel + jnp.dot(
+                sib_att[part, :], sib_grad[:, across], preferred_element_type=jnp.float32
+            )
+            panel = (scale * panel).astype(jnp.bfloat16)
+            for g in range(group):
+                for s in range(STREAMS):
+                    top = (g * STREAMS + s) * rows
+                    sums[s, place(orders[s], 2 * (first + g), d)] = panel[top : top + rows, :]
+
+    def hop(s, level):
+        size = 2**level
+        mine = slots[s] // size
+        theirs = mine + 1 - 2 * (mine % 2)
+        axis, bit = orders[s][level]
+        return remote(
+            sums.at[s, pl.ds(theirs * size, size)],
+            arrived.at[s, pl.ds(size, size)],
+            send_sem.at[s, level],
+            recv_sem.at[s, level],
+            partner(axis, bit),
+        )
+
+    for s in range(STREAMS):
+        hop(s, levels - 1).start()
+    for level in range(levels - 1, -1, -1):
+        size = 2**level
+        for s in range(STREAMS):
+            hop(s, level).wait()
+            start = slots[s] // size * size
+            if level == 0:
+                out_ref[s * rows : (s + 1) * rows, :] = sums[s, slots[s]].astype(
+                    jnp.float32
+                ) + arrived[s, 1].astype(jnp.float32)
+                continue
+
+            @pl.loop(0, size)
+            def _(step):
+                total = sums[s, start + step].astype(jnp.float32) + arrived[
+                    s, size + step
+                ].astype(jnp.float32)
+                sums[s, start + step] = total.astype(jnp.bfloat16)
+
+            hop(s, level - 1).start()
+
+
+def summed_weight_grad(att, grad, scale, seq_count, data_count):
+    rows = 2 * att.shape[1] // seq_count
+    columns = grad.shape[1] // data_count
+    levels = log2(seq_count // 2) + log2(data_count)
+    slots = (STREAMS, 2**levels, rows // STREAMS, columns)
+    vmem = pl.BlockSpec(memory_space=pltpu.VMEM)
+    return pl.pallas_call(
+        functools.partial(weight_grad_kernel, seq_count, data_count, scale),
+        out_shape=jax.ShapeDtypeStruct((rows, columns), jnp.float32),
+        in_specs=[vmem] * 2,
+        out_specs=vmem,
+        scratch_shapes=[
+            pltpu.VMEM(slots, jnp.bfloat16),
+            pltpu.VMEM(slots, jnp.bfloat16),
+            pltpu.VMEM(att.shape[1:], jnp.bfloat16),
+            pltpu.VMEM(grad.shape, jnp.bfloat16),
+            pltpu.SemaphoreType.DMA((STREAMS, levels)),
+            pltpu.SemaphoreType.DMA((STREAMS, levels)),
+            pltpu.SemaphoreType.DMA((2,)),
+            pltpu.SemaphoreType.DMA((2,)),
+        ],
+        compiler_params=pltpu.CompilerParams(
+            collective_id=1, has_side_effects=True, vmem_limit_bytes=40 << 20
+        ),
+        cost_estimate=pl.CostEstimate(
+            flops=4 * att.size * grad.shape[1],
+            bytes_accessed=150 << 20,
+            transcendentals=0,
+        ),
+    )(att, grad)
 
 
 def shards(queries, key_rows, value_rows, out_grad, out_weight):
@@ -43,14 +280,10 @@
     col_ids = lax.broadcasted_iota(jnp.int32, (tokens_dev, tokens_dev), 1)
     causal = (row_ids >= col_ids).astype(jnp.float32)
     kv_local = jnp.einsum("shd,she->hde", key_h, value_h, preferred_element_type=jnp.float32)
-    wide_weight = lax.all_gather(out_weight, "dp", axis=1, tiled=True)
-    head_grad = lax.dot_general(
-        grad_flat,
-        lax.all_gather(wide_weight, "seq", axis=0, tiled=True),
-        (((1,), (1,)), ((), ())),
-        preferred_element_type=jnp.float32,
-    ).astype(jnp.bfloat16)
-    grad_h = head_grad.reshape(tokens_dev, HEADS, HEAD)
+    grad_h = gathered_head_grad(out_weight, grad_flat, seq_devices, data_devices)
+    feature_rows = out_weight.shape[0]
+    grad_h = grad_h.reshape(2, tokens_dev, seq_devices // 2, feature_rows)
+    grad_h = grad_h.transpose(1, 2, 0, 3).reshape(tokens_dev, HEADS, HEAD)
     query_dout = jnp.einsum("thd,the->hde", query_h, grad_h, preferred_element_type=jnp.float32)
     prefix_scaled = exchanged_sums(kv_local, score_scale, "seq", False)
     suffix_scaled = exchanged_sums(query_dout, score_scale, "seq", True)
@@ -63,21 +296,11 @@
     attended = attended + jnp.einsum(
         "thd,hde->the", query_h, prefix_scaled, preferred_element_type=jnp.float32
     )
-    attended = attended.astype(jnp.bfloat16).reshape(tokens_dev, HD)
-    row_sums = lax.psum_scatter(
-        (
-            grad_scale
-            * lax.dot_general(
-                attended, grad_flat, (((0,), (0,)), ((), ())), preferred_element_type=jnp.float32
-            )
-        ).astype(jnp.bfloat16),
-        "seq",
-        scatter_dimension=0,
-        tiled=True,
-    )
-    weight_grad = lax.psum_scatter(row_sums, "dp", scatter_dimension=1, tiled=True).astype(
-        jnp.float32
-    )
+    attended = attended.astype(jnp.bfloat16).reshape(
+        tokens_dev, seq_devices // 2, 2, feature_rows
+    )
+    attended = attended.transpose(2, 1, 3, 0).reshape(2, HD // 2, tokens_dev)
+    weight_grad = summed_weight_grad(attended, grad_flat, grad_scale, seq_devices, data_devices)
     grad_scores = (
         score_scale
         * jnp.einsum("the,she->hts", grad_h, value_h, preferred_element_type=jnp.float32)

time: 320 us -> 220 us (0.69)
  waiting for transfers between devices: 203 us -> 14.8 us
  Pallas kernels: 0 us -> 132 us
  other arithmetic: 13.8 us -> 0.02 us
  between operations: 14 us -> 0.84 us
  blocking collectives: 10.6 us -> 0 us
  matrix products: 40.6 us -> 32.5 us
    pallas_call x0 -> x2, Pallas kernels: none -> 132 us  [the longest x1 72.4 us: gathered_head_grad(): pl.pallas_call(functools.partial(head_grad_kernel, seq_count, data_count)...]
    reduce_scatter x2 -> x0, waiting for transfers between devices: 93.4 us -> none  [the longest x1 93.4 us: shards(): lax.psum_scatter((grad_scale * lax.dot_general(attended, grad_flat, (((0,...]
    all_gather x1 -> x0, waiting for transfers between devices: 76.8 us -> none  [shards(): lax.all_gather(wide_weight, 'seq', axis=0, tiled=True)]
    all_to_all x2, waiting for transfers between devices: 21.1 us -> 8.77 us  [exchanged_sums(): mine = lax.all_to_all(rows, axis, 0, 0, tiled=True)]
    all_gather x1 -> x0, blocking collectives: 10.6 us -> none  [shards(): wide_weight = lax.all_gather(out_weight, 'dp', axis=1, tiled=True)]
    dot_general x2, matrix products: 12.3 us -> 2.9 us  [exchanged_sums(): jnp.dot(ahead.astype(jnp.bfloat16), mine, preferred_element_type=jnp.floa...]
    unnamed x29 -> x0, other arithmetic: 9.13 us -> none
    all_to_all x2, waiting for transfers between devices: 11.3 us -> 6.03 us  [exchanged_sums(): back = lax.all_to_all(sums, axis, 0, 0, tiled=True)]
  transfers between devices with their start and end apart: 7 -> 4, of which waited for: 6 -> 3; matrix products, arithmetic and copies ran while one was open for 11% -> 16% of each run, Pallas kernels for 0% -> 33%
where the time goes in v2:
time: 220 us; the launch traced here: 219 us
  Pallas kernels  132 us (60%)
  matrix products  32.5 us (15%)
  starting transfers between devices  20.3 us (9%)
  local copies, waits for them, and re-layouts  18.8 us (9%)
  waiting for transfers between devices  14.8 us (7%)
    pallas_call x1, Pallas kernels, gathered_head_grad(): pl.pallas_call(functools.partial(head_grad_kernel, seq_count, data_count)...  72.4 us
    pallas_call x1, Pallas kernels, summed_weight_grad(): pl.pallas_call(functools.partial(weight_grad_kernel, seq_count, data_coun...  59.5 us
    all_to_all x2, starting transfers between devices, exchanged_sums(): mine = lax.all_to_all(rows, axis, 0, 0, tiled=True)  11.7 us
    unnamed x31, local copies, waits for them, and re-layouts  11.6 us
    all_to_all x2, waiting for transfers between devices, exchanged_sums(): mine = lax.all_to_all(rows, axis, 0, 0, tiled=True)  8.77 us
    all_to_all x2, starting transfers between devices, exchanged_sums(): back = lax.all_to_all(sums, axis, 0, 0, tiled=True)  8.67 us
    all_to_all x2, waiting for transfers between devices, exchanged_sums(): back = lax.all_to_all(sums, axis, 0, 0, tiled=True)  6.03 us
  transfers between devices with their start and end apart: 4, of which 3 were waited for; matrix products, arithmetic and copies ran while one was open for 16% of the time, Pallas kernels for 33%

profile of v2, /device:TPU:0, one launch (start us, length us, event | category | flops | bytes accessed | tf_op | source)
XLA Modules:
  0.0 219.2 jit_solution(10442687759209351584)
XLA Ops:
  0.6 1.6 copy.56
  2.5 1.3 convolution_convert_fusion.1
  3.8 7.4 %all-to-all-start = ((bf16[16,128,128]{2,1,0:T(8,128)(2,1)}), bf16[16,128,128]{2,1,0:T(8,128)(2,1)}, u32[]{:S(2)}, u32[]{:S(2)}) async-start(bf16[16,128,128]{2,1,0:T(8,128)(2,1)} %convolution_convert_fusion.1), calls=%async_computation | async-start | bytes 1048576 | tf_op jit(solution)/shard_map/all_to_all | solution.py:20
  11.2 72.4 %shard_map.84 = bf16[2,256,1024]{2,1,0:T(8,128)(2,1)S(1)} custom-call(bf16[128,1024]{1,0:T(8,128)(2,1)S(1)} %copy-done.1, bf16[256,2048]{1,0:T(8,128)(2,1)S(1)} %bitcast.78), custom_call_target="tpu_custom_call" | custom-call | flops 2147483648 | bytes 157286400 | tf_op jit(solution)/shard_map/pallas_call | solution.py:131
  83.9 1.0 bitcast_bitcast_fusion
  85.0 2.4 %copy.30 = bf16[256,8,2,128]{0,3,2,1:T(8,128)(2,1)} copy(bf16[256,8,2,128]{3,1,0,2:T(8,128)(2,1)} %bitcast_bitcast_fusion) | data formatting | bytes 2097152 | tf_op jit(solution)/shard_map/transpose | solution.py:286
  87.4 1.5 copy.61
  88.9 1.0 copy-done.2
  90.0 1.3 fusion.5
  91.2 4.2 %all-to-all-start.2 = ((bf16[16,128,128]{1,2,0:T(8,128)(2,1)}), bf16[16,128,128]{1,2,0:T(8,128)(2,1)}, u32[]{:S(2)}, u32[]{:S(2)}) async-start(bf16[16,128,128]{1,2,0:T(8,128)(2,1)} %fusion.5), calls=%async_computation.2 | async-start | bytes 1048576 | tf_op jit(solution)/shard_map/all_to_all | solution.py:20
  95.5 3.3 %multiply_convert_fusion.1 = bf16[16,256,256]{2,1,0:T(8,128)(2,1)} fusion(bf16[256,16,128]{0,2,1:T(8,128)(2,1)} %bitcast.92, bf16[256,16,128]{0,2,1:T(8,128)(2,1)S(1)} %bitcast.85, f32[256,256]{1,0:T(8,128)S(1)} %fusion.22), kind=kOutput, calls=%fused_computation.5 | convolution fusion | flops 270532608 | bytes 4456448 | tf_op jit(solution)/shard_map/the,she->hts/dot_general | solution.py:306
  98.8 1.4 fusion.7
  101.2 8.8 %all-to-all-done.2 = bf16[16,128,128]{1,2,0:T(8,128)(2,1)} async-done(((bf16[16,128,128]{1,2,0:T(8,128)(2,1)}), bf16[16,128,128]{1,2,0:T(8,128)(2,1)}, u32[]{:S(2)}, u32[]{:S(2)}) %all-to-all-start.2) | async-done | bytes 524320 | tf_op jit(solution)/shard_map/all_to_all | solution.py:20
  109.9 4.2 %all-to-all-start.1 = ((bf16[16,128,128]{2,1,0:T(8,128)(2,1)}), bf16[16,128,128]{2,1,0:T(8,128)(2,1)}, u32[]{:S(2)}, u32[]{:S(2)}) async-start(bf16[16,128,128]{2,1,0:T(8,128)(2,1)} %bitcast.101), calls=%async_computation.1 | async-start | bytes 1048576 | tf_op jit(solution)/shard_map/all_to_all | solution.py:26
  114.2 3.5 %multiply_convert_fusion = bf16[16,256,256]{2,1,0:T(8,128)(2,1)} fusion(f32[256,256]{1,0:T(8,128)S(1)} %fusion.22, bf16[256,16,128]{2,1,0:T(8,128)(2,1)S(1)} %bitcast.81, bf16[256,16,128]{2,1,0:T(8,128)(2,1)} %bitcast.89), kind=kOutput, calls=%fused_computation.4 | convolution fusion | flops 270532608 | bytes 4456448 | tf_op jit(solution)/shard_map/thd,shd->hts/dot_general | solution.py:292
  117.7 2.2 fusion.9
  119.8 1.9 fusion.13
  121.7 2.0 copy.39
  123.8 1.4 fusion.6
  126.1 2.5 %all-to-all-done.1 = bf16[16,128,128]{2,1,0:T(8,128)(2,1)} async-done(((bf16[16,128,128]{2,1,0:T(8,128)(2,1)}), bf16[16,128,128]{2,1,0:T(8,128)(2,1)}, u32[]{:S(2)}, u32[]{:S(2)}) %all-to-all-start.1) | async-done | bytes 524320 | tf_op jit(solution)/shard_map/all_to_all | solution.py:26
  128.7 4.4 %all-to-all-start.3 = ((bf16[16,128,128]{2,1,0:T(8,128)(2,1)}), bf16[16,128,128]{2,1,0:T(8,128)(2,1)}, u32[]{:S(2)}, u32[]{:S(2)}) async-start(bf16[16,128,128]{2,1,0:T(8,128)(2,1)} %bitcast.102), calls=%async_computation.3 | async-start | bytes 1048576 | tf_op jit(solution)/shard_map/all_to_all | solution.py:26
  133.1 3.9 %fusion.23 = f32[16,128,256]{2,1,0:T(8,128)} fusion(bf16[256,16,128]{0,2,1:T(8,128)(2,1)} %bitcast.93, bf16[16,256,256]{2,1,0:T(8,128)(2,1)} %multiply_convert_fusion), kind=kOutput, calls=%fused_computation.37 | convolution fusion | flops 268435456 | bytes 5242880 | tf_op jit(solution)/shard_map/hts,the->she/dot_general | solution.py:317
  137.0 2.2 %fusion.24 = f32[16,256,128]{1,2,0:T(8,128)} fusion(bf16[16,256,256]{2,1,0:T(8,128)(2,1)S(1)} %copy-done.7, bf16[256,16,128]{0,2,1:T(8,128)(2,1)S(1)} %bitcast.86), kind=kOutput, calls=%fused_computation.38 | convolution fusion | flops 268435456 | bytes 5242880 | tf_op jit(solution)/shard_map/hts,shd->thd/dot_general | solution.py:295
  139.2 2.5 %fusion.4 = bf16[256,16,128]{0,2,1:T(8,128)(2,1)} fusion(f32[16,256,128]{1,2,0:T(8,128)S(1)} %copy-done.9, bf16[16,128,128]{2,1,0:T(8,128)(2,1)} %all-to-all-done.1, bf16[256,16,128]{0,2,1:T(8,128)(2,1)S(1)} %bitcast.95), kind=kOutput, calls=%fused_computation.11 | convolution fusion | flops 135266304 | bytes 4718592 | tf_op jit(solution)/shard_map/the,hde->thd/dot_general | solution.py:310
  141.6 2.3 %copy.49 = bf16[1,256,2048]{2,1,0:T(8,128)(2,1)} copy(bf16[1,256,2048]{1,2,0:T(8,128)(2,1)} %bitcast.99) | data formatting | bytes 2097152
  143.9 3.5 %all-to-all-done.3 = bf16[16,128,128]{2,1,0:T(8,128)(2,1)} async-done(((bf16[16,128,128]{2,1,0:T(8,128)(2,1)}), bf16[16,128,128]{2,1,0:T(8,128)(2,1)}, u32[]{:S(2)}, u32[]{:S(2)}) %all-to-all-start.3) | async-done | bytes 524320 | tf_op jit(solution)/shard_map/all_to_all | solution.py:26
  147.4 3.2 %fusion.3 = bf16[256,16,128]{0,2,1:T(8,128)(2,1)} fusion(f32[16,256,128]{1,2,0:T(8,128)} %fusion.13, bf16[16,128,128]{2,1,0:T(8,128)(2,1)} %all-to-all-done.3, bf16[256,16,128]{0,2,1:T(8,128)(2,1)S(1)} %bitcast.87), kind=kOutput, calls=%fused_computation.9 | convolution fusion | flops 135266304 | bytes 4718592 | tf_op jit(solution)/shard_map/she,hde->shd/dot_general | solution.py:314
  150.5 2.3 %copy.50 = bf16[1,256,2048]{2,1,0:T(8,128)(2,1)} copy(bf16[1,256,2048]{1,2,0:T(8,128)(2,1)} %bitcast.100) | data formatting | bytes 2097152
  152.8 2.3 %add_convert_fusion = bf16[16,128,256]{2,1,0:T(8,128)(2,1)S(1)} fusion(f32[16,128,256]{2,1,0:T(8,128)} %fusion.23, bf16[16,128,128]{2,1,0:T(8,128)(2,1)} %all-to-all-done.3, bf16[256,16,128]{2,1,0:T(8,128)(2,1)S(1)} %bitcast.83), kind=kOutput, calls=%fused_computation.12 | convolution fusion | flops 135266304 | bytes 4718592 | tf_op jit(solution)/shard_map/shd,hde->she/dot_general | solution.py:318
  155.1 1.4 copy.51
  156.5 2.3 %fusion.2 = bf16[256,16,128]{0,2,1:T(8,128)(2,1)S(1)} fusion(f32[16,256,128]{1,2,0:T(8,128)} %fusion.24, bf16[16,128,128]{2,1,0:T(8,128)(2,1)} %all-to-all-done.1, bf16[256,16,128]{2,1,0:T(8,128)(2,1)S(1)} %bitcast.91), kind=kOutput, calls=%fused_computation.7 | convolution fusion | flops 135266304 | bytes 4718592 | tf_op jit(solution)/shard_map/thd,hde->the/dot_general | solution.py:296
  158.9 59.5 %shard_map.85 = f32[128,1024]{1,0:T(8,128)S(1)} custom-call(bf16[2,1024,256]{2,1,0:T(8,128)(2,1)S(1)} %bitcast.76, bf16[256,2048]{1,0:T(8,128)(2,1)S(1)} %bitcast.79), custom_call_target="tpu_custom_call" | custom-call | flops 4294967296 | bytes 157286400 | tf_op jit(solution)/shard_map/pallas_call | solution.py:240
  (29 shorter events, 3.2 us)
Async XLA Ops:
  0.6 1.6 copy-start.10
  2.5 8.8 %copy-start = (bf16[1,256,2048]{2,1,0:T(8,128)(2,1)S(1)}, bf16[1,256,2048]{2,1,0:T(8,128)(2,1)}, u32[]{:S(2)}) copy-start(bf16[1,256,2048]{2,1,0:T(8,128)(2,1)} %param.8) | copy-start | bytes 3145732
  2.5 8.8 %copy-start.1 = (bf16[128,1024]{1,0:T(8,128)(2,1)S(1)}, bf16[128,1024]{1,0:T(8,128)(2,1)}, u32[]{:S(2)}) copy-start(bf16[128,1024]{1,0:T(8,128)(2,1)} %weight_ref.1) | copy-start | bytes 786436
  3.8 87.5 %all-to-all-start = ((bf16[16,128,128]{2,1,0:T(8,128)(2,1)}), bf16[16,128,128]{2,1,0:T(8,128)(2,1)}, u32[]{:S(2)}, u32[]{:S(2)}) async-start(bf16[16,128,128]{2,1,0:T(8,128)(2,1)} %convolution_convert_fusion.1), calls=%async_computation | async-start | bytes 1048576 | tf_op jit(solution)/shard_map/all_to_all | solution.py:20
  87.4 2.6 %copy-start.5 = (bf16[256,8,2,128]{0,3,2,1:T(8,128)(2,1)S(1)}, bf16[256,8,2,128]{0,3,2,1:T(8,128)(2,1)}, u32[]{:S(2)}) copy-start(bf16[256,8,2,128]{0,3,2,1:T(8,128)(2,1)} %copy.30) | copy-start | bytes 3145732
  88.9 1.0 copy-start.2
  91.2 18.7 %all-to-all-start.2 = ((bf16[16,128,128]{1,2,0:T(8,128)(2,1)}), bf16[16,128,128]{1,2,0:T(8,128)(2,1)}, u32[]{:S(2)}, u32[]{:S(2)}) async-start(bf16[16,128,128]{1,2,0:T(8,128)(2,1)} %fusion.5), calls=%async_computation.2 | async-start | bytes 1048576 | tf_op jit(solution)/shard_map/all_to_all | solution.py:20
  109.9 18.7 %all-to-all-start.1 = ((bf16[16,128,128]{2,1,0:T(8,128)(2,1)}), bf16[16,128,128]{2,1,0:T(8,128)(2,1)}, u32[]{:S(2)}, u32[]{:S(2)}) async-start(bf16[16,128,128]{2,1,0:T(8,128)(2,1)} %bitcast.101), calls=%async_computation.1 | async-start | bytes 1048576 | tf_op jit(solution)/shard_map/all_to_all | solution.py:26
  114.2 3.5 %copy-start.8 = (bf16[16,256,256]{2,1,0:T(8,128)(2,1)S(1)}, bf16[16,256,256]{2,1,0:T(8,128)(2,1)}, u32[]{:S(2)}) copy-start(bf16[16,256,256]{2,1,0:T(8,128)(2,1)} %multiply_convert_fusion.1) | copy-start | bytes 6291460
  117.7 2.2 copy-start.3
  128.7 18.7 %all-to-all-start.3 = ((bf16[16,128,128]{2,1,0:T(8,128)(2,1)}), bf16[16,128,128]{2,1,0:T(8,128)(2,1)}, u32[]{:S(2)}, u32[]{:S(2)}) async-start(bf16[16,128,128]{2,1,0:T(8,128)(2,1)} %bitcast.102), calls=%async_computation.3 | async-start | bytes 1048576 | tf_op jit(solution)/shard_map/all_to_all | solution.py:26
  133.1 3.9 %copy-start.7 = (bf16[16,256,256]{2,1,0:T(8,128)(2,1)S(1)}, bf16[16,256,256]{2,1,0:T(8,128)(2,1)}, u32[]{:S(2)}) copy-start(bf16[16,256,256]{2,1,0:T(8,128)(2,1)} %multiply_convert_fusion) | copy-start | bytes 6291460
  137.0 2.2 %copy-start.6 = (bf16[256,8,2,128]{0,3,2,1:T(8,128)(2,1)S(1)}, bf16[256,8,2,128]{0,3,2,1:T(8,128)(2,1)}, u32[]{:S(2)}) copy-start(bf16[256,8,2,128]{0,3,2,1:T(8,128)(2,1)} %copy.30) | copy-start | bytes 3145732
  137.0 2.2 %copy-start.9 = (f32[16,256,128]{1,2,0:T(8,128)S(1)}, f32[16,256,128]{1,2,0:T(8,128)}, u32[]{:S(2)}) copy-start(f32[16,256,128]{1,2,0:T(8,128)} %fusion.9) | copy-start | bytes 6291460
  155.1 1.4 copy-start.4

commit v3 on v1

v3 whole, which is shorter than its diff:
```python
import functools
import math

import jax
import jax.numpy as jnp
from jax import lax
from jax.experimental import pallas as pl
from jax.experimental.pallas import tpu as pltpu
from jax.sharding import PartitionSpec as P

HEADS = 16
HEAD = 128
HD = 2048


STREAMS = 4
MESH = pl.DeviceIdType.MESH


def log2(count):
    return count.bit_length() - 1


def stream_bits(stream, seq_count, data_count):
    high = [("seq", bit) for bit in range(log2(seq_count) - 1, 0, -1)]
    data = [("dp", bit) for bit in range(log2(data_count))]
    return high[:-1] + data + high[-1:] if stream % 2 else high + data


def place(bits, seq, data):
    index = {"seq": seq, "dp": data}
    return sum((index[axis] // 2**bit) % 2 * 2**level for level, (axis, bit) in enumerate(bits))


def partner(axis, bit):
    index = lax.axis_index(axis)
    return {axis: index + (1 - 2 * ((index // 2**bit) % 2)) * 2**bit}


def greet(seq_count, data_count):
    barrier = pltpu.get_barrier_semaphore()
    bits = [("seq", 0)] + stream_bits(0, seq_count, data_count)
    for axis, bit in bits:
        pl.semaphore_signal(barrier, inc=1, device_id=partner(axis, bit), device_id_type=MESH)
    pl.semaphore_wait(barrier, len(bits))


def remote(src, dst, send, recv, device):
    return pltpu.make_async_remote_copy(
        src_ref=src, dst_ref=dst, send_sem=send, recv_sem=recv, device_id=device, device_id_type=MESH
    )


def contract(left, right, left_dim, right_dim):
    return lax.dot_general(
        left, right, (((left_dim,), (right_dim,)), ((), ())), preferred_element_type=jnp.float32
    )


def sum_steps(part, result, scale, reverse, scratch, seq_count):
    out16, in16, total, before, outs, ins, send_sem, recv_sem = scratch
    seq = lax.axis_index("seq")
    core = seq % 2
    half = before.shape[0]
    own = pl.ds(pl.multiple_of(core * half, half), half)
    other = pl.ds(pl.multiple_of((1 - core) * half, half), half)
    hops = log2(seq_count) - 1

    def flag(bit):
        set_bit = (seq // 2**bit) % 2
        return ((1 - set_bit) if reverse else set_bit).astype(jnp.float32)

    def pair_hop():
        return remote(out16, in16, send_sem.at[0], recv_sem.at[0], partner("seq", 0))

    def chip_hop(level):
        return remote(
            outs.at[level], ins.at[level], send_sem.at[level + 1], recv_sem.at[level + 1],
            partner("seq", level + 1) if level < hops else partner("seq", 0),
        )

    def first():
        out16[...] = part[...].astype(jnp.bfloat16)
        pair_hop().start()

    def second():
        pair_hop().wait()
        total[...] = part[own, :] + in16[own, :].astype(jnp.float32)
        before[...] = jnp.zeros_like(before)
        outs[0] = total[...].astype(jnp.bfloat16)
        chip_hop(0).start()

    def next_hop(level):
        chip_hop(level).wait()
        got = ins[level].astype(jnp.float32)
        before[...] += flag(level + 1) * got
        if level + 1 < hops:
            total[...] += got
            outs[level + 1] = total[...].astype(jnp.bfloat16)
        else:
            outs[level + 1] = before[...].astype(jnp.bfloat16)
        chip_hop(level + 1).start()

    def last():
        chip_hop(hops).wait()
        result[own, :] = (
            scale * (before[...] + flag(0) * in16[own, :].astype(jnp.float32))
        ).astype(jnp.bfloat16)
        result[other, :] = (
            scale
            * (ins[hops].astype(jnp.float32) + flag(0) * in16[other, :].astype(jnp.float32))
        ).astype(jnp.bfloat16)

    return [first, second] + [functools.partial(next_hop, level) for level in range(hops)] + [last]


def kernel(
    seq_count, data_count, score_scale, grad_scale,
    query_ref, key_ref, value_ref, grad_ref, weight_ref,
    query_out, key_out, value_out, weight_out,
    held, sums, arrived, sib_grad, head_grad, away, landed, att, sib_att,
    scores, key_sum, value_sum, part, prefix, suffix,
    out16, in16, total, before, outs, ins,
    gather_send, gather_recv, reduce_send, reduce_recv, pair_send, pair_recv,
    scan_send, scan_recv,
):
    seq, data = lax.axis_index("seq"), lax.axis_index("dp")
    core = seq % 2
    sibling = partner("seq", 0)
    rows, columns = held.shape[2], held.shape[3]
    tokens = grad_ref.shape[0]
    shard_rows = rows * STREAMS
    orders = [stream_bits(s, seq_count, data_count) for s in range(STREAMS)]
    slots = [place(orders[s], seq, data) for s in range(STREAMS)]
    levels = len(orders[0])
    group = max(1, 256 // shard_rows)
    causal = (
        lax.broadcasted_iota(jnp.int32, (tokens, tokens), 0)
        >= lax.broadcasted_iota(jnp.int32, (tokens, tokens), 1)
    ).astype(jnp.float32)

    def head_columns(h):
        return pl.ds(pl.multiple_of(h * HEAD, HEAD), HEAD)

    for s in range(STREAMS):
        held[s, slots[s]] = weight_ref[s * rows : (s + 1) * rows, :]
    greet(seq_count, data_count)

    def gather_hop(s, level):
        size = 2**level
        block = held.at[s, pl.ds(slots[s] // size * size, size)]
        axis, bit = orders[s][level]
        return remote(
            block, block, gather_send.at[s, level], gather_recv.at[s, level], partner(axis, bit)
        )

    def gather_level(level):
        for s in range(STREAMS):
            gather_hop(s, level).wait()
            if level + 1 < levels:
                gather_hop(s, level + 1).start()

    def reduce_hop(s, level):
        size = 2**level
        mine = slots[s] // size
        theirs = mine + 1 - 2 * (mine % 2)
        axis, bit = orders[s][level]
        return remote(
            sums.at[s, pl.ds(theirs * size, size)],
            arrived.at[s, pl.ds(size, size)],
            reduce_send.at[s, level],
            reduce_recv.at[s, level],
            partner(axis, bit),
        )

    def reduce_level(level):
        size = 2**level
        for s in range(STREAMS):
            reduce_hop(s, level).wait()
            start = slots[s] // size * size
            if level == 0:
                weight_out[s * rows : (s + 1) * rows, :] = sums[s, slots[s]].astype(
                    jnp.float32
                ) + arrived[s, 1].astype(jnp.float32)
                continue

            @pl.loop(0, size)
            def _(step):
                added = sums[s, start + step].astype(jnp.float32) + arrived[
                    s, size + step
                ].astype(jnp.float32)
                sums[s, start + step] = added.astype(jnp.bfloat16)

            reduce_hop(s, level - 1).start()

    def swap(src, dst, index):
        return remote(src, dst, pair_send.at[index], pair_recv.at[index], sibling)

    for s in range(STREAMS):
        gather_hop(s, 0).start()
    grad_swap = swap(grad_ref, sib_grad, 0)
    grad_swap.start()

    @pl.loop(0, HEADS)
    def _(h):
        at = head_columns(h)
        part[at, :] = contract(key_ref[:, at], value_ref[:, at], 0, 0)

    scan = (out16, in16, total, before, outs, ins)
    steps = sum_steps(
        part, prefix, score_scale, False,
        tuple(ref.at[0] for ref in scan + (scan_send, scan_recv)), seq_count,
    )
    steps[0]()

    @pl.loop(0, HEADS)
    def _(h):
        at = head_columns(h)
        scores[h] = (
            score_scale * contract(query_ref[:, at], key_ref[:, at], 1, 1) * causal
        ).astype(jnp.bfloat16)

    for index in range(max(len(steps) - 1, levels - 1)):
        if index + 1 < len(steps):
            steps[index + 1]()
        if index < levels - 1:
            gather_level(index)

    @pl.loop(0, HEADS)
    def _(h):
        at = head_columns(h)
        attended = contract(scores[h], value_ref[:, at], 1, 0)
        attended = attended + contract(query_ref[:, at], prefix[at, :], 1, 0)
        turned = attended.T.astype(jnp.bfloat16)
        pieces = HEAD // shard_rows
        for piece in range(pieces):
            shard = h * pieces + piece
            att[shard % 2, pl.ds(pl.multiple_of(shard // 2 * shard_rows, shard_rows), shard_rows), :] = (
                turned[piece * shard_rows : (piece + 1) * shard_rows, :]
            )

    att_swap = swap(att.at[1 - core], sib_att, 1)
    att_swap.start()
    grad_swap.wait()
    att_swap.wait()
    height = group * shard_rows
    for first in range(0, seq_count // 2, group):
        strip = pl.ds(first * shard_rows, height)
        for d in range(data_count):
            across = slice(d * columns, (d + 1) * columns)
            panel = contract(att[core, strip, :], grad_ref[:, across], 1, 0)
            panel = panel + contract(sib_att[strip, :], sib_grad[:, across], 1, 0)
            panel = (grad_scale * panel).astype(jnp.bfloat16)
            for g in range(group):
                for s in range(STREAMS):
                    top = (g * STREAMS + s) * rows
                    sums[s, place(orders[s], 2 * (first + g), d)] = panel[top : top + rows, :]
    for s in range(STREAMS):
        reduce_hop(s, levels - 1).start()

    gather_level(levels - 1)
    half = away.shape[1]
    for first in range(0, seq_count // 2, group):
        panel = jnp.concatenate(
            [
                jnp.concatenate(
                    [held[s, place(orders[s], 2 * j, d)] for d in range(data_count)], axis=1
                )
                for j in range(first, first + group)
                for s in range(STREAMS)
            ],
            axis=0,
        )
        strip = slice(first * shard_rows, first * shard_rows + height)
        away[:, strip] = contract(sib_grad[...], panel, 1, 1).astype(jnp.bfloat16)
        mine = contract(grad_ref[...], panel, 1, 1).astype(jnp.bfloat16)
        for side in range(2):

            @pl.when(core == side)
            def _():
                for g in range(group):
                    left = (2 * (first + g) + side) * shard_rows
                    head_grad[:, left : left + shard_rows] = mine[
                        :, g * shard_rows : (g + 1) * shard_rows
                    ]

    back = swap(away, landed, 2)
    back.start()
    back.wait()
    for side in range(2):

        @pl.when(core != side)
        def _():
            for j in range(seq_count // 2):
                left = (2 * j + side) * shard_rows
                head_grad[:, left : left + shard_rows] = landed[
                    :, j * shard_rows : (j + 1) * shard_rows
                ]

    @pl.loop(0, HEADS)
    def _(h):
        at = head_columns(h)
        part[at, :] = contract(query_ref[:, at], head_grad[:, at], 0, 0)

    steps = sum_steps(
        part, suffix, score_scale, True,
        tuple(ref.at[1] for ref in scan + (scan_send, scan_recv)), seq_count,
    )
    steps[0]()

    def local_heads(begin, end):
        @pl.loop(begin, end)
        def _(h):
            at = head_columns(h)
            rows_g, rows_q, rows_k = head_grad[:, at], query_ref[:, at], key_ref[:, at]
            grad_scores = (
                score_scale * contract(rows_g, value_ref[:, at], 1, 1) * causal
            ).astype(jnp.bfloat16)
            query_out[:, at] = (
                contract(grad_scores, rows_k, 1, 0) + contract(rows_g, prefix[at, :], 1, 1)
            ).astype(jnp.bfloat16)
            key_sum[:, at] = contract(grad_scores, rows_q, 0, 0)
            value_sum[:, at] = contract(scores[h], rows_g, 0, 0)

    chunks = len(steps) - 1
    for index in range(max(chunks, levels - 1)):
        if index < chunks:
            local_heads(HEADS * index // chunks, HEADS * (index + 1) // chunks)
            steps[index + 1]()
        if index < levels - 1:
            reduce_level(levels - 1 - index)

    @pl.loop(0, HEADS)
    def _(h):
        at = head_columns(h)
        key_out[:, at] = (
            key_sum[:, at] + contract(value_ref[:, at], suffix[at, :], 1, 1)
        ).astype(jnp.bfloat16)
        value_out[:, at] = (
            value_sum[:, at] + contract(key_ref[:, at], suffix[at, :], 1, 0)
        ).astype(jnp.bfloat16)

    reduce_level(0)


def shards(queries, key_rows, value_rows, out_grad, out_weight):
    tokens = queries.shape[1]
    seq_count = lax.axis_size("seq")
    data_count = lax.axis_size("dp")
    seq_length = tokens * seq_count
    score_scale = 1.0 / math.sqrt(HEAD * seq_length)
    grad_scale = 1.0 / math.sqrt(queries.shape[0] * data_count * seq_length)
    features = queries.shape[2]
    shard_rows, columns = out_weight.shape
    width = out_grad.shape[2]
    hops = log2(seq_count // 2)
    levels = hops + log2(data_count)
    bf16, f32 = jnp.bfloat16, jnp.float32
    blocks = (STREAMS, 2**levels, shard_rows // STREAMS, columns)
    half = features // 2
    vmem = pl.BlockSpec(memory_space=pltpu.VMEM)
    dma = pltpu.SemaphoreType.DMA
    flat = jax.ShapeDtypeStruct((tokens, features), bf16)
    query_grad, key_grad, value_grad, weight_grad = pl.pallas_call(
        functools.partial(kernel, seq_count, data_count, score_scale, grad_scale),
        out_shape=(flat, flat, flat, jax.ShapeDtypeStruct((shard_rows, columns), f32)),
        in_specs=[vmem] * 5,
        out_specs=(vmem,) * 4,
        scratch_shapes=[
            pltpu.VMEM(blocks, bf16),
            pltpu.VMEM(blocks, bf16),
            pltpu.VMEM(blocks, bf16),
            pltpu.VMEM((tokens, width), bf16),
            pltpu.VMEM((tokens, features), bf16),
            pltpu.VMEM((tokens, half), bf16),
            pltpu.VMEM((tokens, half), bf16),
            pltpu.VMEM((2, half, tokens), bf16),
            pltpu.VMEM((half, tokens), bf16),
            pltpu.VMEM((HEADS, tokens, tokens), bf16),
            pltpu.VMEM((tokens, features), f32),
            pltpu.VMEM((tokens, features), f32),
            pltpu.VMEM((features, HEAD), f32),
            pltpu.VMEM((features, HEAD), bf16),
            pltpu.VMEM((features, HEAD), bf16),
            pltpu.VMEM((2, features, HEAD), bf16),
            pltpu.VMEM((2, features, HEAD), bf16),
            pltpu.VMEM((2, half, HEAD), f32),
            pltpu.VMEM((2, half, HEAD), f32),
            pltpu.VMEM((2, hops + 1, half, HEAD), bf16),
            pltpu.VMEM((2, hops + 1, half, HEAD), bf16),
            dma((STREAMS, levels)),
            dma((STREAMS, levels)),
            dma((STREAMS, levels)),
            dma((STREAMS, levels)),
            dma((3,)),
            dma((3,)),
            dma((2, hops + 2)),
            dma((2, hops + 2)),
        ],
        compiler_params=pltpu.CompilerParams(
            collective_id=0, has_side_effects=True, vmem_limit_bytes=56 << 20
        ),
    )(queries[0], key_rows[0], value_rows[0], out_grad[0], out_weight)
    return query_grad[None], key_grad[None], value_grad[None], weight_grad


def solution(mesh):
    return jax.shard_map(
        shards,
        mesh=mesh,
        in_specs=(
            P("dp", "seq", None),
            P("dp", "seq", None),
            P("dp", "seq", None),
            P("dp", "seq", None),
            P("seq", "dp"),
        ),
        out_specs=(
            P("dp", "seq", None),
            P("dp", "seq", None),
            P("dp", "seq", None),
            P("seq", "dp"),
        ),
        check_vma=False,
    )
```

time: 320 us -> 136 us (0.42)
  waiting for transfers between devices: 203 us -> 0 us
  Pallas kernels: 0 us -> 129 us
  matrix products: 40.6 us -> 0 us
  starting transfers between devices: 20.5 us -> 0 us
  other arithmetic: 13.8 us -> 0 us
  between operations: 14 us -> 0.65 us
  local copies, waits for them, and re-layouts: 17 us -> 6.19 us
  blocking collectives: 10.6 us -> 0 us
    pallas_call x0 -> x1, Pallas kernels: none -> 129 us  [shards(): pl.pallas_call(functools.partial(kernel, seq_count, data_count, score_sca...]
    reduce_scatter x2 -> x0, waiting for transfers between devices: 93.4 us -> none  [the longest x1 93.4 us: shards(): lax.psum_scatter((grad_scale * lax.dot_general(attended, grad_flat, (((0,...]
    all_gather x1 -> x0, waiting for transfers between devices: 76.8 us -> none  [shards(): lax.all_gather(wide_weight, 'seq', axis=0, tiled=True)]
    dot_general x14 -> x0, matrix products: 40.6 us -> none  [the longest x1 6.71 us: shards(): lax.dot_general(grad_flat, lax.all_gather(wide_weight, 'seq', axis=0, til...]
    all_to_all x4 -> x0, waiting for transfers between devices: 32.4 us -> none  [the longest x2 21.1 us: exchanged_sums(): mine = lax.all_to_all(rows, axis, 0, 0, tiled=True)]
    all_to_all x4 -> x0, starting transfers between devices: 20.4 us -> none  [the longest x2 11.7 us: exchanged_sums(): mine = lax.all_to_all(rows, axis, 0, 0, tiled=True)]
    all_gather x1 -> x0, blocking collectives: 10.6 us -> none  [shards(): wide_weight = lax.all_gather(out_weight, 'dp', axis=1, tiled=True)]
    unnamed x29 -> x0, other arithmetic: 9.13 us -> none
  transfers between devices with their start and end apart: 7 -> 0, of which waited for: 6 -> 0; matrix products, arithmetic and copies ran while one was open for 11% -> 0% of each run, Pallas kernels for 0% -> 0%
where the time goes in v3:
time: 136 us
  Pallas kernels  129 us (95%)
  local copies, waits for them, and re-layouts  6.19 us (5%)
    pallas_call x1, Pallas kernels, shards(): pl.pallas_call(functools.partial(kernel, seq_count, data_count, score_sca...  129 us
    unnamed x10, local copies, waits for them, and re-layouts  6.19 us

profile of v3, /device:TPU:0, one launch (start us, length us, event | category | flops | bytes accessed | tf_op | source)
XLA Modules:
  0.0 136.1 jit_solution(17465269312060269088)
XLA Ops:
  0.6 129.2 %shard_map.84 = (bf16[256,2048]{1,0:T(8,128)(2,1)}, bf16[256,2048]{1,0:T(8,128)(2,1)}, bf16[256,2048]{1,0:T(8,128)(2,1)}, f32[128,1024]{1,0:T(8,128)}) custom-call(bf16[256,2048]{1,0:T(8,128)(2,1)} %bitcast.7, bf16[256,2048]{1,0:T(8,128)(2,1)} %bitcast.8, bf16[256,2048]{1,0:T(8,128)(2,1)} %bitcast.9, bf16[256,2048]{1,0:T(8,128)(2,1)} %bitcast.10, ...), custom_call_target="tpu_custom_call" | custom-call | tf_op jit(solution)/shard_map/pallas_call | solution.py:364
  129.9 0.0 copy-start.1
  129.9 2.4 %copy.13 = bf16[1,256,2048]{2,1,0:T(8,128)(2,1)} copy(bf16[1,256,2048]{2,1,0:T(8,128)(2,1)} %bitcast.13) | data formatting | bytes 2097152
  132.3 0.0 copy-done.1
  132.3 0.0 copy-start
  132.3 1.0 copy.14
  133.3 0.6 copy-done
  133.9 0.0 copy-start.2
  133.9 1.0 copy.15
  134.9 0.4 copy-done.2
  135.3 0.8 copy.16
Async XLA Ops:
  129.9 2.4 %copy-start.1 = (bf16[256,2048]{1,0:T(8,128)(2,1)S(1)}, bf16[256,2048]{1,0:T(8,128)(2,1)}, u32[]{:S(2)}) copy-start(bf16[256,2048]{1,0:T(8,128)(2,1)} %get-tuple-element.9) | copy-start | bytes 3145732
  132.3 1.6 %copy-start = (bf16[256,2048]{1,0:T(8,128)(2,1)S(1)}, bf16[256,2048]{1,0:T(8,128)(2,1)}, u32[]{:S(2)}) copy-start(bf16[256,2048]{1,0:T(8,128)(2,1)} %get-tuple-element.10) | copy-start | bytes 3145732
  133.9 1.4 %copy-start.2 = (f32[128,1024]{1,0:T(8,128)S(1)}, f32[128,1024]{1,0:T(8,128)}, u32[]{:S(2)}) copy-start(f32[128,1024]{1,0:T(8,128)} %get-tuple-element.19) | copy-start | bytes 1572868

commit v4 on v3

--- a/solution.py
+++ b/solution.py
@@ -24,7 +24,8 @@
 def stream_bits(stream, seq_count, data_count):
     high = [("seq", bit) for bit in range(log2(seq_count) - 1, 0, -1)]
     data = [("dp", bit) for bit in range(log2(data_count))]
-    return high[:-1] + data + high[-1:] if stream % 2 else high + data
+    far, near = high[:-1], high[-1:]
+    return [high + data, far + data + near, near + data + far, data + high][stream % 4]
 
 
 def place(bits, seq, data):

time: 136 us -> 132 us (0.971)
  Pallas kernels: 129 us -> 125 us
    pallas_call x1, Pallas kernels: 129 us -> 125 us  [shards(): pl.pallas_call(functools.partial(kernel, seq_count, data_count, score_sca...]
where the time goes in v4:
time: 132 us
  Pallas kernels  125 us (95%)
  local copies, waits for them, and re-layouts  6.19 us (5%)
    pallas_call x1, Pallas kernels, shards(): pl.pallas_call(functools.partial(kernel, seq_count, data_count, score_sca...  125 us
    unnamed x10, local copies, waits for them, and re-layouts  6.19 us

profile of v4, /device:TPU:0, one launch (start us, length us, event | category | flops | bytes accessed | tf_op | source)
XLA Modules:
  0.0 132.0 jit_solution(16399194038181399039)
XLA Ops:
  0.6 125.2 %shard_map.84 = (bf16[256,2048]{1,0:T(8,128)(2,1)}, bf16[256,2048]{1,0:T(8,128)(2,1)}, bf16[256,2048]{1,0:T(8,128)(2,1)}, f32[128,1024]{1,0:T(8,128)}) custom-call(bf16[256,2048]{1,0:T(8,128)(2,1)} %bitcast.7, bf16[256,2048]{1,0:T(8,128)(2,1)} %bitcast.8, bf16[256,2048]{1,0:T(8,128)(2,1)} %bitcast.9, bf16[256,2048]{1,0:T(8,128)(2,1)} %bitcast.10, ...), custom_call_target="tpu_custom_call" | custom-call | tf_op jit(solution)/shard_map/pallas_call | solution.py:365
  125.8 0.0 copy-start.1
  125.8 2.4 %copy.13 = bf16[1,256,2048]{2,1,0:T(8,128)(2,1)} copy(bf16[1,256,2048]{2,1,0:T(8,128)(2,1)} %bitcast.13) | data formatting | bytes 2097152
  128.2 0.0 copy-done.1
  128.2 0.0 copy-start
  128.2 1.0 copy.14
  129.2 0.6 copy-done
  129.8 0.0 copy-start.2
  129.8 1.0 copy.15
  130.8 0.4 copy-done.2
  131.2 0.8 copy.16
Async XLA Ops:
  125.8 2.4 %copy-start.1 = (bf16[256,2048]{1,0:T(8,128)(2,1)S(1)}, bf16[256,2048]{1,0:T(8,128)(2,1)}, u32[]{:S(2)}) copy-start(bf16[256,2048]{1,0:T(8,128)(2,1)} %get-tuple-element.9) | copy-start | bytes 3145732
  128.2 1.6 %copy-start = (bf16[256,2048]{1,0:T(8,128)(2,1)S(1)}, bf16[256,2048]{1,0:T(8,128)(2,1)}, u32[]{:S(2)}) copy-start(bf16[256,2048]{1,0:T(8,128)(2,1)} %get-tuple-element.10) | copy-start | bytes 3145732
  129.8 1.4 %copy-start.2 = (f32[128,1024]{1,0:T(8,128)S(1)}, f32[128,1024]{1,0:T(8,128)}, u32[]{:S(2)}) copy-start(f32[128,1024]{1,0:T(8,128)} %get-tuple-element.19) | copy-start | bytes 1572868

commit v5 on v4

--- a/solution.py
+++ b/solution.py
@@ -56,6 +56,18 @@
     return lax.dot_general(
         left, right, (((left_dim,), (right_dim,)), ((), ())), preferred_element_type=jnp.float32
     )
+
+
+def each_head(begin, end, together, body):
+    whole = begin + (end - begin) // together * together
+
+    @pl.loop(begin, whole, step=together)
+    def _(h):
+        for store in [body(h + i) for i in range(together)]:
+            store()
+
+    for store in [body(h) for h in range(whole, end)]:
+        store()
 
 
 def sum_steps(part, result, scale, reverse, scratch, seq_count):
@@ -141,7 +153,7 @@
     ).astype(jnp.float32)
 
     def head_columns(h):
-        return pl.ds(pl.multiple_of(h * HEAD, HEAD), HEAD)
+        return pl.ds(h * HEAD if isinstance(h, int) else pl.multiple_of(h * HEAD, HEAD), HEAD)
 
     for s in range(STREAMS):
         held[s, slots[s]] = weight_ref[s * rows : (s + 1) * rows, :]
@@ -202,10 +214,15 @@
     grad_swap = swap(grad_ref, sib_grad, 0)
     grad_swap.start()
 
-    @pl.loop(0, HEADS)
-    def _(h):
-        at = head_columns(h)
-        part[at, :] = contract(key_ref[:, at], value_ref[:, at], 0, 0)
+    def store(ref, index, value):
+        ref[index] = value
+
+    def key_value(h):
+        at = head_columns(h)
+        product = contract(key_ref[:, at], value_ref[:, at], 0, 0)
+        return functools.partial(store, part, (at, slice(None)), product)
+
+    each_head(0, HEADS, 4, key_value)
 
     scan = (out16, in16, total, before, outs, ins)
     steps = sum_steps(
@@ -214,12 +231,12 @@
     )
     steps[0]()
 
-    @pl.loop(0, HEADS)
-    def _(h):
-        at = head_columns(h)
-        scores[h] = (
-            score_scale * contract(query_ref[:, at], key_ref[:, at], 1, 1) * causal
-        ).astype(jnp.bfloat16)
+    def head_scores(h):
+        at = head_columns(h)
+        product = score_scale * contract(query_ref[:, at], key_ref[:, at], 1, 1) * causal
+        return functools.partial(store, scores, h, product.astype(jnp.bfloat16))
+
+    each_head(0, HEADS, 4, head_scores)
 
     for index in range(max(len(steps) - 1, levels - 1)):
         if index + 1 < len(steps):
@@ -227,18 +244,24 @@
         if index < levels - 1:
             gather_level(index)
 
-    @pl.loop(0, HEADS)
-    def _(h):
+    def head_attended(h):
         at = head_columns(h)
         attended = contract(scores[h], value_ref[:, at], 1, 0)
         attended = attended + contract(query_ref[:, at], prefix[at, :], 1, 0)
         turned = attended.T.astype(jnp.bfloat16)
         pieces = HEAD // shard_rows
-        for piece in range(pieces):
-            shard = h * pieces + piece
-            att[shard % 2, pl.ds(pl.multiple_of(shard // 2 * shard_rows, shard_rows), shard_rows), :] = (
-                turned[piece * shard_rows : (piece + 1) * shard_rows, :]
-            )
+
+        def put():
+            for piece in range(pieces):
+                shard = h * pieces + piece
+                top = pl.multiple_of(shard // 2 * shard_rows, shard_rows)
+                att[shard % 2, pl.ds(top, shard_rows), :] = turned[
+                    piece * shard_rows : (piece + 1) * shard_rows, :
+                ]
+
+        return put
+
+    each_head(0, HEADS, 4, head_attended)
 
     att_swap = swap(att.at[1 - core], sib_att, 1)
     att_swap.start()
@@ -298,10 +321,12 @@
                     :, j * shard_rows : (j + 1) * shard_rows
                 ]
 
-    @pl.loop(0, HEADS)
-    def _(h):
-        at = head_columns(h)
-        part[at, :] = contract(query_ref[:, at], head_grad[:, at], 0, 0)
+    def query_dout(h):
+        at = head_columns(h)
+        product = contract(query_ref[:, at], head_grad[:, at], 0, 0)
+        return functools.partial(store, part, (at, slice(None)), product)
+
+    each_head(0, HEADS, 4, query_dout)
 
     steps = sum_steps(
         part, suffix, score_scale, True,
@@ -309,37 +334,43 @@
     )
     steps[0]()
 
-    def local_heads(begin, end):
-        @pl.loop(begin, end)
-        def _(h):
-            at = head_columns(h)
-            rows_g, rows_q, rows_k = head_grad[:, at], query_ref[:, at], key_ref[:, at]
-            grad_scores = (
-                score_scale * contract(rows_g, value_ref[:, at], 1, 1) * causal
-            ).astype(jnp.bfloat16)
-            query_out[:, at] = (
-                contract(grad_scores, rows_k, 1, 0) + contract(rows_g, prefix[at, :], 1, 1)
-            ).astype(jnp.bfloat16)
-            key_sum[:, at] = contract(grad_scores, rows_q, 0, 0)
-            value_sum[:, at] = contract(scores[h], rows_g, 0, 0)
+    def local_head(h):
+        at = head_columns(h)
+        rows_g, rows_q, rows_k = head_grad[:, at], query_ref[:, at], key_ref[:, at]
+        grad_scores = (
+            score_scale * contract(rows_g, value_ref[:, at], 1, 1) * causal
+        ).astype(jnp.bfloat16)
+        queried = contract(grad_scores, rows_k, 1, 0) + contract(rows_g, prefix[at, :], 1, 1)
+        keyed = contract(grad_scores, rows_q, 0, 0)
+        valued = contract(scores[h], rows_g, 0, 0)
+
+        def put():
+            query_out[:, at] = queried.astype(jnp.bfloat16)
+            key_sum[:, at] = keyed
+            value_sum[:, at] = valued
+
+        return put
 
     chunks = len(steps) - 1
     for index in range(max(chunks, levels - 1)):
         if index < chunks:
-            local_heads(HEADS * index // chunks, HEADS * (index + 1) // chunks)
+            each_head(HEADS * index // chunks, HEADS * (index + 1) // chunks, 4, local_head)
             steps[index + 1]()
         if index < levels - 1:
             reduce_level(levels - 1 - index)
 
-    @pl.loop(0, HEADS)
-    def _(h):
-        at = head_columns(h)
-        key_out[:, at] = (
-            key_sum[:, at] + contract(value_ref[:, at], suffix[at, :], 1, 1)
-        ).astype(jnp.bfloat16)
-        value_out[:, at] = (
-            value_sum[:, at] + contract(key_ref[:, at], suffix[at, :], 1, 0)
-        ).astype(jnp.bfloat16)
+    def last_terms(h):
+        at = head_columns(h)
+        keyed = key_sum[:, at] + contract(value_ref[:, at], suffix[at, :], 1, 1)
+        valued = value_sum[:, at] + contract(key_ref[:, at], suffix[at, :], 1, 0)
+
+        def put():
+            key_out[:, at] = keyed.astype(jnp.bfloat16)
+            value_out[:, at] = valued.astype(jnp.bfloat16)
+
+        return put
+
+    each_head(0, HEADS, 4, last_terms)
 
     reduce_level(0)
 

time: 132 us -> 128 us (0.970)
  Pallas kernels: 125 us -> 121 us
    pallas_call x1, Pallas kernels: 125 us -> 121 us  [shards(): pl.pallas_call(functools.partial(kernel, seq_count, data_count, score_sca...]
where the time goes in v5:
time: 128 us
  Pallas kernels  121 us (95%)
  local copies, waits for them, and re-layouts  6.19 us (5%)
    pallas_call x1, Pallas kernels, shards(): pl.pallas_call(functools.partial(kernel, seq_count, data_count, score_sca...  121 us
    unnamed x10, local copies, waits for them, and re-layouts  6.19 us

profile of v5, /device:TPU:0, one launch (start us, length us, event | category | flops | bytes accessed | tf_op | source)
XLA Modules:
  0.0 127.9 jit_solution(4423940737094729446)
XLA Ops:
  0.6 121.1 %shard_map.84 = (bf16[256,2048]{1,0:T(8,128)(2,1)}, bf16[256,2048]{1,0:T(8,128)(2,1)}, bf16[256,2048]{1,0:T(8,128)(2,1)}, f32[128,1024]{1,0:T(8,128)}) custom-call(bf16[256,2048]{1,0:T(8,128)(2,1)} %bitcast.7, bf16[256,2048]{1,0:T(8,128)(2,1)} %bitcast.8, bf16[256,2048]{1,0:T(8,128)(2,1)} %bitcast.9, bf16[256,2048]{1,0:T(8,128)(2,1)} %bitcast.10, ...), custom_call_target="tpu_custom_call" | custom-call | tf_op jit(solution)/shard_map/pallas_call | solution.py:396
  121.7 0.0 copy-start.1
  121.7 2.4 %copy.13 = bf16[1,256,2048]{2,1,0:T(8,128)(2,1)} copy(bf16[1,256,2048]{2,1,0:T(8,128)(2,1)} %bitcast.13) | data formatting | bytes 2097152
  124.1 0.0 copy-done.1
  124.1 0.0 copy-start
  124.1 1.0 copy.14
  125.1 0.6 copy-done
  125.7 0.0 copy-start.2
  125.7 1.0 copy.15
  126.7 0.4 copy-done.2
  127.1 0.8 copy.16
Async XLA Ops:
  121.7 2.4 %copy-start.1 = (bf16[256,2048]{1,0:T(8,128)(2,1)S(1)}, bf16[256,2048]{1,0:T(8,128)(2,1)}, u32[]{:S(2)}) copy-start(bf16[256,2048]{1,0:T(8,128)(2,1)} %get-tuple-element.9) | copy-start | bytes 3145732
  124.1 1.6 %copy-start = (bf16[256,2048]{1,0:T(8,128)(2,1)S(1)}, bf16[256,2048]{1,0:T(8,128)(2,1)}, u32[]{:S(2)}) copy-start(bf16[256,2048]{1,0:T(8,128)(2,1)} %get-tuple-element.10) | copy-start | bytes 3145732
  125.7 1.4 %copy-start.2 = (f32[128,1024]{1,0:T(8,128)S(1)}, f32[128,1024]{1,0:T(8,128)}, u32[]{:S(2)}) copy-start(f32[128,1024]{1,0:T(8,128)} %get-tuple-element.19) | copy-start | bytes 1572868
